TPU v7x, 256 devices: a whole 4x4x8 slice. The times are simulated.
256 devices in a mesh: group: 32 (over y_hi, z, core), tok: 8 (over x, y_lo).
Axes of the slice: x: 4, y: 4 (y_hi: 2, y_lo: 2; y = y_hi * 2 + y_lo), z: 8, core: 2. Of those that a mesh axis runs over, the one named last changes fastest.
Arguments:
- latents: bfloat16 [32768, 5120], P(('group', 'tok')), may hold values from -6 to 6
- timesteps: int32 [32], P('group'), may hold values from 0 to 999
- mod_shift: float32 [5120], replicated, may hold values from -3 to 3
- mod_scale: float32 [5120], replicated, may hold values from -1.5 to 1.5
- w_query: bfloat16 [5120, 3072], P('group', 'tok'), may hold values from -7 to 7
- w_key: bfloat16 [5120, 3072], P('group', 'tok'), may hold values from -7 to 7
- w_value: bfloat16 [5120, 3072], P('group', 'tok'), may hold values from -0.078125 to 0.078125
- query_gain: float32 [3072], P('tok'), may hold values from 0.5 to 1.5
- key_gain: float32 [3072], P('tok'), may hold values from 0.5 to 1.5
- cache_keys: bfloat16 [32768, 3072], P('group', 'tok'), may hold values from -85 to 85
- cache_values: bfloat16 [32768, 3072], P('group', 'tok'), may hold values from -6 to 6
- owners: int32 [32], replicated, may hold values from 0 to 31, each once
- tile_mask: int32 [24, 8, 24], P('tok'), may hold values from 0 to 1, as said below
Outputs:
- attended: bfloat16 [32768, 3072], P('group', 'tok')
Inputs may be any that keep to these rules, and one draw needn't show every extreme that they name: `tile_mask`: each query tile i of each head sees 1 to 8 key tiles, always tile 2 * 8 + i; some query tile sees exactly 8.
All inputs are finite; a program needn't handle non-finite values.
Results may differ from a plain program's by a relative error of at most 0.012.
The roundings to bfloat16 on the way count: a program that leaves them out, or rounds other values in their place, can miss the bound.
Values may be sent and summed in bfloat16 or wider, within the bound.
No kernel may reach another device: no remote copies, remote signals or barrier semaphores. Data moves between devices by JAX's collectives and lax.ppermute only.
A program may use at most 128 MiB of HBM per device.

v0:
```python
import functools
import math

import jax
import jax.numpy as jnp
from jax import lax
from jax.experimental import pallas as pl
from jax.experimental.pallas import tpu as pltpu
from jax.sharding import PartitionSpec as P


EPSILON = 1e-06
TILE = 128
MOST = 8
FAR = -1e30
NY, NZ, NC, NX = 2, 8, 2, 4
SLOT_OF = (0, 1, 3, 5, 6, 7, 2, 4)
INTERPRET = False


def group_shift(value, dz=0, dc=0, dy=0):
    def at(y, z, c):
        return (y % NY) * NZ * NC + (z % NZ) * NC + c % NC

    route = [
        (at(y, z, c), at(y + dy, z + dz, c + dc))
        for y in range(NY)
        for z in range(NZ)
        for c in range(NC)
    ]
    return lax.ppermute(value, "group", route)


def tok_shift(value, dx=0, dy=0):
    route = [
        (x * 2 + y, ((x + dx) % NX) * 2 + (y + dy) % 2) for x in range(NX) for y in range(2)
    ]
    return lax.ppermute(value, "tok", route)


def from_behind(block, axis, distance):
    devices = range(lax.axis_size(axis))
    route = [(i - distance, i) for i in devices if i - distance in devices]
    return lax.ppermute(block, axis, route)


def modulate(rows_block, timestep, mod_shift, mod_scale):
    values = rows_block.astype(jnp.float32)
    width = values.shape[-1]
    centred = values - jnp.mean(values, axis=-1, keepdims=True)
    spread = jnp.mean(centred * centred, axis=-1, keepdims=True)
    normed = centred * lax.rsqrt(spread + EPSILON)
    freqs = jnp.exp(-math.log(10000.0) * jnp.arange(width, dtype=jnp.float32) / width)
    angles = timestep.astype(jnp.float32) * freqs
    return (
        normed * (1.0 + mod_scale + 0.5 * jnp.cos(angles)) + mod_shift + 0.5 * jnp.sin(angles)
    ).astype(jnp.bfloat16)


def scaled_rows(raw, squares, width, gain):
    return (raw * lax.rsqrt(squares / width + EPSILON)[:, None] * gain).astype(jnp.bfloat16)


def gather_tokens(own):
    half = own.shape[0] // 2

    def move(value, dx, dy=0):
        return tok_shift(value, dx, dy)

    beside = move(own, 0, 1)
    own_lo = move(own, 1)
    own_hi = move(own, -1)
    far_a = move(own_lo[:half], 1)
    far_b = move(own_hi[half:], -1)
    side_lo = move(beside, 1)
    side_hi = move(beside, -1)
    far_c = move(side_lo[:half], 1)
    far_d = move(side_hi[half:], -1)
    return (own, beside, own_lo, own_hi, side_lo, side_hi, far_a, far_b, far_c, far_d)


def fold_kernel(orders, held, *refs):
    came, out = refs[:-1], refs[-1]
    for slot in range(held.shape[0]):
        total = held[slot : slot + 1, :]
        for ref, order in zip(came, orders):
            total = total + ref[order[slot] : order[slot] + 1, :]
        out[slot : slot + 1, :] = total


def fold(value, shifts):
    orders = []
    for dx, dy in shifts:
        picks = [0] * (2 * NX)
        for n, slot in enumerate(SLOT_OF):
            picks[slot] = SLOT_OF[((n // 2 + dx) % NX) * 2 + (n % 2 + dy) % 2]
        orders.append(tuple(picks))
    came = [tok_shift(value, dx, dy) for dx, dy in shifts]
    return pl.pallas_call(
        functools.partial(fold_kernel, tuple(orders)),
        out_shape=jax.ShapeDtypeStruct(value.shape, value.dtype),
        interpret=INTERPRET,
        name="fold",
    )(value, *came)


def sum_over_tok(value):
    tiles = value.reshape(2 * NX, -1)
    pair = fold(tiles, ((0, 1),))
    return fold(pair, ((1, 0), (3, 0), (2, 0))).reshape(-1)


def swap_z(value, distance):
    def at(y, z, c):
        return y * NZ * NC + z * NC + c

    route = [
        (at(y, z, c), at(y, z ^ distance, c))
        for y in range(NY)
        for z in range(NZ)
        for c in range(NC)
    ]
    return lax.ppermute(value, "group", route)


def spread_cache(cache_keys, cache_values, root):
    me = lax.axis_index("group")
    moves = (
        (0, lambda v: group_shift(v, dc=1)),
        (4, lambda v: group_shift(v, dy=1)),
        (3, lambda v: swap_z(v, 4)),
        (2, lambda v: swap_z(v, 2)),
        (1, lambda v: swap_z(v, 1)),
    )
    low, high = cache_keys, cache_values
    for bit, move in moves:
        mine, theirs = (me >> bit) & 1, (root >> bit) & 1
        kept = jnp.where(mine == 1, high, low)
        sent = jnp.where(mine == 1, low, high)
        came = move(sent)
        held = jnp.where(mine == theirs, kept, came)
        half = held.shape[0] // 2
        low, high = held[:half], held[half:]
    for bit, move in moves[::-1]:
        mine = (me >> bit) & 1
        came = move(held)
        low, high = jnp.where(mine == 1, came, held), jnp.where(mine == 1, held, came)
        if bit:
            held = jnp.concatenate([low, high], axis=0)
    return low, high


def gather_weights(own):
    depth = own.shape[0]
    beside = group_shift(own, dy=1)
    pair = jnp.concatenate([own, beside], axis=0)
    low, high = [pair], [pair]
    for _ in range(1, NZ // 2):
        low.append(group_shift(low[-1], dz=1))
        high.append(group_shift(high[-1], dz=-1))
    own_half, beside_half = low[-1][:depth], high[-1][depth:]
    far_own = group_shift(own_half, dz=1)
    far_beside = group_shift(beside_half, dz=-1)
    me = lax.axis_index("group")
    y, z, c = me >> 4, (me >> 1) & (NZ - 1), me & 1

    def at(dy, dz, dc):
        return ((y ^ dy) << 4) | (((z + dz) & (NZ - 1)) << 1) | (c ^ dc)

    held = [(pair, ((0, 0), (1, 0)))]
    for k in range(1, NZ // 2):
        held.append((low[k], ((0, -k), (1, -k))))
        held.append((high[k], ((0, k), (1, k))))
    held.append((far_own, ((0, NZ // 2),)))
    held.append((far_beside, ((1, NZ // 2),)))
    pieces, places = [], []
    for dc in range(NC):
        for piece, where in held:
            pieces.append(piece if dc == 0 else group_shift(piece, dc=1))
            places += [at(dy, dz, dc) for dy, dz in where]
    return assemble(pieces, jnp.stack(places), depth)


def assemble_kernel(depth, places, *refs):
    pieces, out, sem = refs[:-2], refs[-2], refs[-1]
    copies = []
    for piece in pieces:
        for n in range(piece.shape[0] // depth):
            row = pl.multiple_of(places[len(copies)] * depth, depth)
            copies.append(
                pltpu.make_async_copy(
                    piece.at[pl.ds(n * depth, depth)],
                    out.at[pl.ds(row, depth)],
                    sem.at[len(copies)],
                )
            )
    for copy in copies:
        copy.start()
    for copy in copies:
        copy.wait()


def assemble(pieces, places, depth):
    columns = pieces[0].shape[1]
    rows = places.shape[0] * depth
    anywhere = pl.BlockSpec(memory_space=pl.ANY)
    return pl.pallas_call(
        functools.partial(assemble_kernel, depth),
        grid_spec=pltpu.PrefetchScalarGridSpec(
            num_scalar_prefetch=1,
            grid=(),
            in_specs=[anywhere] * len(pieces),
            out_specs=anywhere,
            scratch_shapes=[pltpu.SemaphoreType.DMA((places.shape[0],))],
        ),
        out_shape=jax.ShapeDtypeStruct((rows, columns), pieces[0].dtype),
        cost_estimate=pl.CostEstimate(
            flops=0, transcendentals=0, bytes_accessed=4 * rows * columns
        ),
        interpret=INTERPRET,
        name="assemble",
    )(places, *pieces)


def attend_kernel(
    heads, scale, order, count, slots, query, ck, cv, ek, ev, nk, nv, out, keys, values, sems
):
    span = ck.shape[0]
    parts = ((ck, cv), (ek, ev), (nk, nv))
    copies = []
    for n, (k_part, v_part) in enumerate(parts):
        rows = pl.ds(n * span, span)
        copies.append(pltpu.make_async_copy(k_part, keys.at[rows], sems.at[2 * n]))
        copies.append(pltpu.make_async_copy(v_part, values.at[rows], sems.at[2 * n + 1]))
    for copy in copies:
        copy.start()
    for copy in copies:
        copy.wait()
    tiles = span // TILE

    def few_tiles(first, pairs):
        low = lax.broadcasted_iota(jnp.int32, (1, 2 * TILE), 1) < TILE
        for h in range(heads):
            for i in (first, first + 1):
                one_tile(h, i, pairs, low)

    def one_tile(h, i, pairs, low):
        from_row = pl.multiple_of(slots[i] * TILE, TILE)
        to_row = pl.multiple_of(i * TILE, TILE)
        cols = pl.ds(h * TILE, TILE)
        at = h * tiles + i
        seen = count[at]
        q = query[pl.ds(from_row, TILE), cols]
        scores, vals = [], []
        for p in range(pairs):
            rows = [
                pl.ds(pl.multiple_of(order[at * MOST + 2 * p + s] * TILE, TILE), TILE)
                for s in range(2)
            ]
            k_pair = jnp.concatenate([keys[r, cols] for r in rows], axis=0)
            vals.append(jnp.concatenate([values[r, cols] for r in rows], axis=0))
            s = lax.dot_general(
                q, k_pair, (((1,), (1,)), ((), ())), preferred_element_type=jnp.float32
            )
            bias = jnp.where(
                low,
                jnp.where(2 * p < seen, 0.0, FAR),
                jnp.where(2 * p + 1 < seen, 0.0, FAR),
            )
            scores.append(s * scale + bias)
        top = scores[0]
        for s in scores[1:]:
            top = jnp.maximum(top, s)
        peak = jnp.max(top, axis=1, keepdims=True)
        total, summed = None, None
        for s, v in zip(scores, vals):
            probs = jnp.exp(s - peak)
            total = probs if total is None else total + probs
            added = jnp.dot(probs.astype(jnp.bfloat16), v, preferred_element_type=jnp.float32)
            summed = added if summed is None else summed + added
        denominator = jnp.sum(total, axis=1, keepdims=True)
        out[pl.ds(to_row, TILE), cols] = (summed / denominator).astype(jnp.bfloat16)

    @pl.loop(0, tiles // 2)
    def _(step):
        first = 2 * step
        most = count[first]
        for h in range(heads):
            for n in range(2):
                most = jnp.maximum(most, count[h * tiles + first + n])
        for pairs in range(2, MOST // 2 + 1):
            pl.when(jnp.maximum((most + 1) // 2, 2) == pairs)(functools.partial(few_tiles, first, pairs))


def attend(query, parts, order, count, slots, heads):
    rows, width = query.shape
    anywhere = pl.BlockSpec(memory_space=pl.ANY)
    whole = pl.BlockSpec(memory_space=pltpu.VMEM)
    return pl.pallas_call(
        functools.partial(attend_kernel, heads, 1.0 / math.sqrt(width // heads)),
        grid_spec=pltpu.PrefetchScalarGridSpec(
            num_scalar_prefetch=3,
            grid=(),
            in_specs=[whole] + [anywhere] * 6,
            out_specs=whole,
            scratch_shapes=[
                pltpu.VMEM((3 * rows, width), jnp.bfloat16),
                pltpu.VMEM((3 * rows, width), jnp.bfloat16),
                pltpu.SemaphoreType.DMA((6,)),
            ],
        ),
        out_shape=jax.ShapeDtypeStruct((rows, width), jnp.bfloat16),
        cost_estimate=pl.CostEstimate(
            flops=4 * rows * width * MOST * TILE,
            transcendentals=rows * heads * MOST * TILE,
            bytes_accessed=16 * rows * width,
        ),
        interpret=INTERPRET,
        name="attend",
    )(order, count, slots, query, *parts)


def tile_lists(tile_mask, is_first, tok):
    tiles, key_tiles = tile_mask.shape[1], tile_mask.shape[2]
    ids = jnp.arange(key_tiles, dtype=jnp.int32)
    earlier = (ids >= tiles) & (ids < 2 * tiles)
    allowed = jnp.where(earlier[None, None, :] & is_first, 0, tile_mask)
    count = jnp.sum(allowed, axis=-1)
    upto = (ids[None, :] <= ids[:, None]).astype(jnp.int32)
    rank = jnp.sum(allowed[:, :, None, :] * upto, axis=-1)
    places = jnp.arange(tiles, dtype=jnp.int32)
    step = (((places >> 1) - (tok >> 1)) & (NX - 1)) * 2 + ((places ^ tok) & 1)
    slots = sum(jnp.where(step == n, slot, 0) for n, slot in enumerate(SLOT_OF))
    physical = jnp.concatenate([places, tiles + slots, 2 * tiles + slots])
    turn = jnp.arange(1, MOST + 1, dtype=jnp.int32)
    picked = (rank[:, :, None, :] == turn[None, None, :, None]) & (allowed[:, :, None, :] > 0)
    order = jnp.sum(jnp.where(picked, physical, 0), axis=-1)
    return order.reshape(-1), count.reshape(-1), slots


def local(
    latents,
    timesteps,
    mod_shift,
    mod_scale,
    w_query,
    w_key,
    w_value,
    query_gain,
    key_gain,
    cache_keys,
    cache_values,
    owners,
    tile_mask,
):
    head_cols = w_query.shape[1]
    width = head_cols * lax.axis_size("tok")
    heads = tile_mask.shape[0]
    root = owners[owners.shape[0] - 1]
    modulated = modulate(latents, timesteps[0], mod_shift, mod_scale)
    joined = gather_weights(jnp.concatenate([w_key, w_value, w_query], axis=1))
    tokens = jnp.concatenate(gather_tokens(modulated), axis=0)
    cached_keys, cached_values = spread_cache(cache_keys, cache_values, root)
    order, count, slots = tile_lists(
        tile_mask, lax.axis_index("group") == 0, lax.axis_index("tok")
    )
    both = jnp.dot(tokens, joined[:, : 2 * head_cols], preferred_element_type=jnp.float32)
    raw_key = both[:, :head_cols]
    value_rows = both[:, head_cols:].astype(jnp.bfloat16)
    earlier_values = from_behind(value_rows, "group", 1)
    key_squares = sum_over_tok(jnp.sum(raw_key * raw_key, axis=1))
    raw_query = jnp.dot(tokens, joined[:, 2 * head_cols :], preferred_element_type=jnp.float32)
    key_rows = scaled_rows(raw_key, key_squares, width, key_gain)
    earlier_keys = from_behind(key_rows, "group", 1)
    query_squares = sum_over_tok(jnp.sum(raw_query * raw_query, axis=1))
    query_rows = scaled_rows(raw_query, query_squares, width, query_gain)
    parts = (cached_keys, cached_values, earlier_keys, earlier_values, key_rows, value_rows)
    return attend(query_rows, parts, order, count, slots, heads)


def solution(mesh):
    return jax.shard_map(
        local,
        mesh=mesh,
        in_specs=(
            P(("group", "tok"), None),
            P("group"),
            P(),
            P(),
            P("group", "tok"),
            P("group", "tok"),
            P("group", "tok"),
            P("tok"),
            P("tok"),
            P("group", "tok"),
            P("group", "tok"),
            P(),
            P("tok", None, None),
        ),
        out_specs=P("group", "tok"),
        check_vma=False,
    )
```

profile of v0, /device:TPU:1, one launch (start us, length us, event | category | flops | bytes accessed | tf_op | source)
XLA Modules:
  0.0 626.3 jit_solution(12789056898756592301)
XLA Ops:
  14.2 2.7 collective-permute-start.9
  22.6 33.5 %collective-permute-done.32 = bf16[512,384]{1,0:T(8,128)(2,1)S(1)} collective-permute-done((bf16[512,384]{1,0:T(8,128)(2,1)S(1)}, bf16[512,384]{1,0:T(8,128)(2,1)S(1)}, u32[]{:S(2)}, u32[]{:S(2)}) %collective-permute-start.32) | collective-permute-done | bytes 393248 | tf_op jit(solution)/shard_map/ppermute | solution.py:31
  56.3 7.0 %collective-permute-start.33 = (bf16[256,384]{1,0:T(8,128)(2,1)S(1)}, bf16[256,384]{1,0:T(8,128)(2,1)S(1)}, u32[]{:S(2)}, u32[]{:S(2)}) collective-permute-start(bf16[256,384]{1,0:T(8,128)(2,1)S(1)} %broadcast_select_fusion.8), channel_id=1, source_target_pairs={{0,64},{8,72},{16,80},{24,88},{32,96},{40,104},{48,112},{56,120},{... | collective-permute-start | bytes 589832 | tf_op jit(solution)/shard_map/ppermute | solution.py:123
  63.3 3.7 collective-permute-done.33
  67.1 6.7 %collective-permute-start.34 = (bf16[128,384]{1,0:T(8,128)(2,1)S(1)}, bf16[128,384]{1,0:T(8,128)(2,1)S(1)}, u32[]{:S(2)}, u32[]{:S(2)}) collective-permute-start(bf16[128,384]{1,0:T(8,128)(2,1)S(1)} %broadcast_select_fusion.11), channel_id=1, source_target_pairs={{0,32},{8,40},{16,48},{24,56},{32,0},{40,8},{48,16},{56,24},{64,96... | collective-permute-start | bytes 294920 | tf_op jit(solution)/shard_map/ppermute | solution.py:123
  79.0 13.5 %collective-permute-done.35 = bf16[64,384]{1,0:T(8,128)(2,1)S(1)} collective-permute-done((bf16[64,384]{1,0:T(8,128)(2,1)S(1)}, bf16[64,384]{1,0:T(8,128)(2,1)S(1)}, u32[]{:S(2)}, u32[]{:S(2)}) %collective-permute-start.35) | collective-permute-done | bytes 49184 | tf_op jit(solution)/shard_map/ppermute | solution.py:123
  104.3 13.1 %collective-permute-done.37 = bf16[128,384]{1,0:T(8,128)(2,1)S(1)} collective-permute-done((bf16[128,384]{1,0:T(8,128)(2,1)S(1)}, bf16[128,384]{1,0:T(8,128)(2,1)S(1)}, u32[]{:S(2)}, u32[]{:S(2)}) %collective-permute-start.37) | collective-permute-done | bytes 98336 | tf_op jit(solution)/shard_map/ppermute | solution.py:123
  117.5 6.2 collective-permute-start.38
  127.3 2.8 collective-permute-start.4
  134.7 6.6 %collective-permute-done.39 = bf16[512,384]{1,0:T(8,128)(2,1)S(1)} collective-permute-done((bf16[512,384]{1,0:T(8,128)(2,1)S(1)}, bf16[512,384]{1,0:T(8,128)(2,1)S(1)}, u32[]{:S(2)}, u32[]{:S(2)}) %collective-permute-start.39) | collective-permute-done | bytes 393248 | tf_op jit(solution)/shard_map/ppermute | solution.py:31
  141.3 6.2 collective-permute-start.18
  154.3 3.3 collective-permute-start.6
  158.9 6.2 collective-permute-start.21
  165.1 3.1 collective-permute-done.5
  169.2 2.8 collective-permute-start.8
  172.8 5.6 collective-permute-start.22
  181.4 2.9 collective-permute-done.7
  193.0 359.4 %assemble.1 = bf16[5120,1152]{1,0:T(8,128)(2,1)} custom-call(s32[32]{0:T(128)} %stack.131.places, bf16[320,1152]{1,0:T(8,128)(2,1)} %copy-done.5, bf16[320,1152]{1,0:T(8,128)(2,1)} %copy-done.9, bf16[320,1152]{1,0:T(8,128)(2,1)} %copy-done.11, bf16[320,1152]{1,0:T(8,128)(2,1)} %copy-done.13, bf16[320,1152]{1,0:T(8,128)(2,1)} %copy-done.14, ...), custom_call_target="tpu_custom_call" | custom-call | bytes 23592960 | tf_op jit(solution)/shard_map/assemble/pallas_call | solution.py:207
  552.4 12.2 %fusion = f32[1024,768]{1,0:T(8,128)S(1)} fusion(bf16[1024,5120]{1,0:T(8,128)(2,1)} %constant_dynamic-update-slice_fusion, bf16[5120,1152]{1,0:T(8,128)(2,1)} %assemble.1), kind=kOutput, calls=%fused_computation | convolution fusion | flops 8053063680 | bytes 21495808 | tf_op jit(solution)/shard_map/dot_general | solution.py:367
  565.0 11.1 %multiply_reduce_fusion.1 = (f32[1024]{0:T(1024)}, f32[1024,384]{0,1:T(8,128)}) fusion(bf16[1024,5120]{1,0:T(8,128)(2,1)} %constant_dynamic-update-slice_fusion, bf16[5120,1152]{1,0:T(8,128)(2,1)} %assemble.1), kind=kOutput, calls=%fused_computation.17 | convolution fusion | flops 4027317248 | bytes 15994880 | tf_op jit(solution)/shard_map/dot_general | solution.py:372
  579.1 2.7 collective-permute-start.43
  587.2 2.8 collective-permute-start.46
  599.4 2.9 collective-permute-start.45
  611.5 14.3 %attend.1 = bf16[1024,384]{1,0:T(8,128)(2,1)} custom-call(s32[192]{0:T(256)} %reshape.113.order, s32[24]{0:T(128)} %reshape.114.count, s32[8]{0:T(128)} %copy-done.33, bf16[1024,384]{1,0:T(8,128)(2,1)} %multiply_convert_fusion.1.query, bf16[1024,384]{1,0:T(8,128)(2,1)} %get-tuple-element.12.ck, bf16[1024,384]{1,0:T(8,128)(2,1)} %get-tuple-element.11.cv, ...), custom_call_target="tpu_custom_call" | custom-call | flops 1610612736 | bytes 6291456 | tf_op jit(solution)/shard_map/attend/pallas_call | solution.py:299
  (216 shorter events, 89.8 us)
Async XLA Ops:
  6.7 93.7 %collective-permute-start = (bf16[128,5120]{1,0:T(8,128)(2,1)}, bf16[128,5120]{1,0:T(8,128)(2,1)}, u32[]{:S(2)}, u32[]{:S(2)}) collective-permute-start(bf16[128,5120]{1,0:T(8,128)(2,1)} %get-tuple-element.6), channel_id=1, source_target_pairs={{0,1},{1,0},{2,3},{3,2},{4,5},{5,4},{6,7},{7,6},{8,9},{9,8},{10,11... | collective-permute-start | bytes 3932168 | tf_op jit(solution)/shard_map/ppermute | solution.py:38
  8.8 108.7 %collective-permute-start.1 = (bf16[128,5120]{1,0:T(8,128)(2,1)}, bf16[128,5120]{1,0:T(8,128)(2,1)}, u32[]{:S(2)}, u32[]{:S(2)}) collective-permute-start(bf16[128,5120]{1,0:T(8,128)(2,1)} %get-tuple-element.6), channel_id=1, source_target_pairs={{0,2},{1,3},{2,4},{3,5},{4,6},{5,7},{6,0},{7,1},{8,10},{9,11},{10,... | collective-permute-start | bytes 3932168 | tf_op jit(solution)/shard_map/ppermute | solution.py:38
  14.2 59.6 %collective-permute-start.9 = (bf16[160,1152]{1,0:T(8,128)(2,1)S(1)}, bf16[160,1152]{1,0:T(8,128)(2,1)}, u32[]{:S(2)}, u32[]{:S(2)}) collective-permute-start(bf16[160,1152]{1,0:T(8,128)(2,1)S(1)} %constant_dynamic-update-slice_fusion.10), channel_id=1, source_target_pairs={{0,128},{8,136},{16,144},{24,152},{32,160},{40,168},{48,176},{56,1... | collective-permute-start | bytes 1105928 | tf_op jit(solution)/shard_map/ppermute | solution.py:31
  19.1 37.0 %collective-permute-start.32 = (bf16[512,384]{1,0:T(8,128)(2,1)S(1)}, bf16[512,384]{1,0:T(8,128)(2,1)S(1)}, u32[]{:S(2)}, u32[]{:S(2)}) collective-permute-start(bf16[512,384]{1,0:T(8,128)(2,1)S(1)} %broadcast_select_fusion.5), channel_id=1, source_target_pairs={{0,128},{8,136},{16,144},{24,152},{32,160},{40,168},{48,176},{56,1... | collective-permute-start | bytes 1179656 | tf_op jit(solution)/shard_map/ppermute | solution.py:31
  74.9 20.4 %collective-permute-start.10 = (bf16[320,1152]{1,0:T(8,128)(2,1)S(1)}, bf16[320,1152]{1,0:T(8,128)(2,1)S(1)}, u32[]{:S(2)}, u32[]{:S(2)}) collective-permute-start(bf16[320,1152]{1,0:T(8,128)(2,1)S(1)} %pad_maximum_fusion.1.refs_0_), channel_id=1, source_target_pairs={{0,16},{8,24},{16,32},{24,40},{32,48},{40,56},{48,64},{56,72},{64,... | collective-permute-start | bytes 2211848 | tf_op jit(solution)/shard_map/ppermute | solution.py:31
  75.0 22.8 %collective-permute-start.11 = (bf16[320,1152]{1,0:T(8,128)(2,1)S(1)}, bf16[320,1152]{1,0:T(8,128)(2,1)S(1)}, u32[]{:S(2)}, u32[]{:S(2)}) collective-permute-start(bf16[320,1152]{1,0:T(8,128)(2,1)S(1)} %pad_maximum_fusion.1.refs_0_), channel_id=1, source_target_pairs={{0,112},{8,120},{16,0},{24,8},{32,16},{40,24},{48,32},{56,40},{64,... | collective-permute-start | bytes 2211848 | tf_op jit(solution)/shard_map/ppermute | solution.py:31
  95.2 32.1 %collective-permute-start.2 = (bf16[128,5120]{1,0:T(8,128)(2,1)}, bf16[128,5120]{1,0:T(8,128)(2,1)S(1)}, u32[]{:S(2)}, u32[]{:S(2)}) collective-permute-start(bf16[128,5120]{1,0:T(8,128)(2,1)} %get-tuple-element.6), channel_id=1, source_target_pairs={{0,6},{1,7},{2,0},{3,1},{4,2},{5,3},{6,4},{7,5},{8,14},{9,15},{10,... | collective-permute-start | bytes 3932168 | tf_op jit(solution)/shard_map/ppermute | solution.py:38
  97.7 32.4 %collective-permute-start.12 = (bf16[320,1152]{1,0:T(8,128)(2,1)S(1)}, bf16[320,1152]{1,0:T(8,128)(2,1)S(1)}, u32[]{:S(2)}, u32[]{:S(2)}) collective-permute-start(bf16[320,1152]{1,0:T(8,128)(2,1)S(1)} %collective-permute-done.10.refs_1_), channel_id=1, source_target_pairs={{0,16},{8,24},{16,32},{24,40},{32,48},{40,56},{48,64},{56,72},{64,... | collective-permute-start | bytes 2211848 | tf_op jit(solution)/shard_map/ppermute | solution.py:31
  97.8 32.4 %collective-permute-start.13 = (bf16[320,1152]{1,0:T(8,128)(2,1)S(1)}, bf16[320,1152]{1,0:T(8,128)(2,1)S(1)}, u32[]{:S(2)}, u32[]{:S(2)}) collective-permute-start(bf16[320,1152]{1,0:T(8,128)(2,1)S(1)} %collective-permute-done.11.refs_2_), channel_id=1, source_target_pairs={{0,112},{8,120},{16,0},{24,8},{32,16},{40,24},{48,32},{56,40},{64,... | collective-permute-start | bytes 2211848 | tf_op jit(solution)/shard_map/ppermute | solution.py:31
  100.4 17.0 %collective-permute-start.37 = (bf16[128,384]{1,0:T(8,128)(2,1)S(1)}, bf16[128,384]{1,0:T(8,128)(2,1)S(1)}, u32[]{:S(2)}, u32[]{:S(2)}) collective-permute-start(bf16[128,384]{1,0:T(8,128)(2,1)S(1)} %pad_maximum_fusion.4), channel_id=1, source_target_pairs={{0,32},{8,40},{16,48},{24,56},{32,0},{40,8},{48,16},{56,24},{64,96... | collective-permute-start | bytes 294920 | tf_op jit(solution)/shard_map/ppermute | solution.py:123
  117.4 33.6 %collective-permute-start.3 = (bf16[128,5120]{1,0:T(8,128)(2,1)}, bf16[128,5120]{1,0:T(8,128)(2,1)S(1)}, u32[]{:S(2)}, u32[]{:S(2)}) collective-permute-start(bf16[128,5120]{1,0:T(8,128)(2,1)} %collective-permute-done), channel_id=1, source_target_pairs={{0,2},{1,3},{2,4},{3,5},{4,6},{5,7},{6,0},{7,1},{8,10},{9,11},{10,... | collective-permute-start | bytes 3932168 | tf_op jit(solution)/shard_map/ppermute | solution.py:38
  127.3 27.0 %collective-permute-start.4 = (bf16[128,5120]{1,0:T(8,128)(2,1)}, bf16[128,5120]{1,0:T(8,128)(2,1)S(1)}, u32[]{:S(2)}, u32[]{:S(2)}) collective-permute-start(bf16[128,5120]{1,0:T(8,128)(2,1)} %collective-permute-done), channel_id=1, source_target_pairs={{0,6},{1,7},{2,0},{3,1},{4,2},{5,3},{6,4},{7,5},{8,14},{9,15},{10,... | collective-permute-start | bytes 3932168 | tf_op jit(solution)/shard_map/ppermute | solution.py:38
  130.1 19.2 %collective-permute-start.14 = (bf16[320,1152]{1,0:T(8,128)(2,1)S(1)}, bf16[320,1152]{1,0:T(8,128)(2,1)S(1)}, u32[]{:S(2)}, u32[]{:S(2)}) collective-permute-start(bf16[320,1152]{1,0:T(8,128)(2,1)S(1)} %collective-permute-done.12.refs_3_), channel_id=1, source_target_pairs={{0,16},{8,24},{16,32},{24,40},{32,48},{40,56},{48,64},{56,72},{64,... | collective-permute-start | bytes 2211848 | tf_op jit(solution)/shard_map/ppermute | solution.py:31
  130.3 20.6 %collective-permute-start.15 = (bf16[320,1152]{1,0:T(8,128)(2,1)S(1)}, bf16[320,1152]{1,0:T(8,128)(2,1)S(1)}, u32[]{:S(2)}, u32[]{:S(2)}) collective-permute-start(bf16[320,1152]{1,0:T(8,128)(2,1)S(1)} %collective-permute-done.13.refs_4_), channel_id=1, source_target_pairs={{0,112},{8,120},{16,0},{24,8},{32,16},{40,24},{48,32},{56,40},{64,... | collective-permute-start | bytes 2211848 | tf_op jit(solution)/shard_map/ppermute | solution.py:31
  141.3 17.5 %collective-permute-start.18 = (bf16[320,1152]{1,0:T(8,128)(2,1)S(1)}, bf16[320,1152]{1,0:T(8,128)(2,1)S(1)}, u32[]{:S(2)}, u32[]{:S(2)}) collective-permute-start(bf16[320,1152]{1,0:T(8,128)(2,1)S(1)} %pad_maximum_fusion.1.refs_0_), channel_id=1, source_target_pairs={{0,8},{8,0},{16,24},{24,16},{32,40},{40,32},{48,56},{56,48},{64,72... | collective-permute-start | bytes 2211848 | tf_op jit(solution)/shard_map/ppermute | solution.py:31
  149.4 19.7 %collective-permute-start.19 = (bf16[320,1152]{1,0:T(8,128)(2,1)S(1)}, bf16[320,1152]{1,0:T(8,128)(2,1)S(1)}, u32[]{:S(2)}, u32[]{:S(2)}) collective-permute-start(bf16[320,1152]{1,0:T(8,128)(2,1)S(1)} %copy-done.10), channel_id=1, source_target_pairs={{0,8},{8,0},{16,24},{24,16},{32,40},{40,32},{48,56},{56,48},{64,72... | collective-permute-start | bytes 2211848 | tf_op jit(solution)/shard_map/ppermute | solution.py:31
  150.9 21.9 %collective-permute-start.20 = (bf16[320,1152]{1,0:T(8,128)(2,1)S(1)}, bf16[320,1152]{1,0:T(8,128)(2,1)S(1)}, u32[]{:S(2)}, u32[]{:S(2)}) collective-permute-start(bf16[320,1152]{1,0:T(8,128)(2,1)S(1)} %copy-done.12), channel_id=1, source_target_pairs={{0,8},{8,0},{16,24},{24,16},{32,40},{40,32},{48,56},{56,48},{64,72... | collective-permute-start | bytes 2211848 | tf_op jit(solution)/shard_map/ppermute | solution.py:31
  151.1 17.1 %collective-permute-start.5 = (bf16[64,5120]{1,0:T(8,128)(2,1)S(1)}, bf16[64,5120]{1,0:T(8,128)(2,1)S(1)}, u32[]{:S(2)}, u32[]{:S(2)}) collective-permute-start(bf16[64,5120]{1,0:T(8,128)(2,1)S(1)} %slice.77), channel_id=1, source_target_pairs={{0,2},{1,3},{2,4},{3,5},{4,6},{5,7},{6,0},{7,1},{8,10},{9,11},{10,... | collective-permute-start | bytes 1966088 | tf_op jit(solution)/shard_map/ppermute | solution.py:38
  158.9 19.6 %collective-permute-start.21 = (bf16[320,1152]{1,0:T(8,128)(2,1)S(1)}, bf16[320,1152]{1,0:T(8,128)(2,1)S(1)}, u32[]{:S(2)}, u32[]{:S(2)}) collective-permute-start(bf16[320,1152]{1,0:T(8,128)(2,1)S(1)} %collective-permute-done.12.refs_3_), channel_id=1, source_target_pairs={{0,8},{8,0},{16,24},{24,16},{32,40},{40,32},{48,56},{56,48},{64,72... | collective-permute-start | bytes 2211848 | tf_op jit(solution)/shard_map/ppermute | solution.py:31
  168.1 16.2 %collective-permute-start.7 = (bf16[64,5120]{1,0:T(8,128)(2,1)S(1)}, bf16[64,5120]{1,0:T(8,128)(2,1)S(1)}, u32[]{:S(2)}, u32[]{:S(2)}) collective-permute-start(bf16[64,5120]{1,0:T(8,128)(2,1)S(1)} %slice.79), channel_id=1, source_target_pairs={{0,2},{1,3},{2,4},{3,5},{4,6},{5,7},{6,0},{7,1},{8,10},{9,11},{10,... | collective-permute-start | bytes 1966088 | tf_op jit(solution)/shard_map/ppermute | solution.py:38
  169.2 20.5 %collective-permute-start.8 = (bf16[64,5120]{1,0:T(8,128)(2,1)S(1)}, bf16[64,5120]{1,0:T(8,128)(2,1)S(1)}, u32[]{:S(2)}, u32[]{:S(2)}) collective-permute-start(bf16[64,5120]{1,0:T(8,128)(2,1)S(1)} %slice.80), channel_id=1, source_target_pairs={{0,6},{1,7},{2,0},{3,1},{4,2},{5,3},{6,4},{7,5},{8,14},{9,15},{10,... | collective-permute-start | bytes 1966088 | tf_op jit(solution)/shard_map/ppermute | solution.py:38
  172.8 17.8 %collective-permute-start.22 = (bf16[320,1152]{1,0:T(8,128)(2,1)S(1)}, bf16[320,1152]{1,0:T(8,128)(2,1)S(1)}, u32[]{:S(2)}, u32[]{:S(2)}) collective-permute-start(bf16[320,1152]{1,0:T(8,128)(2,1)S(1)} %collective-permute-done.13.refs_4_), channel_id=1, source_target_pairs={{0,8},{8,0},{16,24},{24,16},{32,40},{40,32},{48,56},{56,48},{64,72... | collective-permute-start | bytes 2211848 | tf_op jit(solution)/shard_map/ppermute | solution.py:31
  190.7 408.7 %collective-permute-start.40 = (bf16[1024,384]{1,0:T(8,128)(2,1)}, bf16[1024,384]{1,0:T(8,128)(2,1)}, u32[]{:S(2)}, u32[]{:S(2)}) collective-permute-start(bf16[1024,384]{1,0:T(8,128)(2,1)} %pad_maximum_fusion), channel_id=1, source_target_pairs={{0,8},{8,0},{16,24},{24,16},{32,40},{40,32},{48,56},{56,48},{64,72... | collective-permute-start | bytes 2359304 | tf_op jit(solution)/shard_map/ppermute | solution.py:31
  587.2 22.5 %collective-permute-start.46 = (bf16[1024,384]{1,0:T(8,128)(2,1)}, bf16[1024,384]{1,0:T(8,128)(2,1)}, u32[]{:S(2)}, u32[]{:S(2)}) collective-permute-start(bf16[1024,384]{1,0:T(8,128)(2,1)} %slice.118.nv), channel_id=1, source_target_pairs={{0,8},{8,16},{16,24},{24,32},{32,40},{40,48},{48,56},{56,64},{64,7... | collective-permute-start | bytes 2359304 | tf_op jit(solution)/shard_map/ppermute | solution.py:44
  (59 other events, 798.1 us)
where the time goes:
time: 638 us; the launch traced here: 626 us
  Pallas kernels  379 us (59%)
  starting transfers between devices  90.8 us (14%)
  waiting for transfers between devices  82.1 us (13%)
  local copies, waits for them, and re-layouts  25.3 us (4%)
  matrix products  23.3 us (4%)
  other arithmetic  20.7 us (3%)
    pallas_call x1, Pallas kernels, assemble(): pl.pallas_call(functools.partial(assemble_kernel, depth), grid_spec=pltpu...  359 us
    ppermute x22, waiting for transfers between devices, group_shift(): return lax.ppermute(value, 'group', route)  42 us
    ppermute x22, starting transfers between devices, group_shift(): return lax.ppermute(value, 'group', route)  38.9 us
    ppermute x6, waiting for transfers between devices, swap_z(): return lax.ppermute(value, 'group', route)  30.3 us
    ppermute x17, starting transfers between devices, tok_shift(): return lax.ppermute(value, 'tok', route)  23.4 us
    ppermute x6, starting transfers between devices, swap_z(): return lax.ppermute(value, 'group', route)  22.9 us
    unnamed x82, local copies, waits for them, and re-layouts  16.8 us
    pallas_call x1, Pallas kernels, attend(): pl.pallas_call(functools.partial(attend_kernel, heads, 1.0 / math.sqrt(wi...  14.3 us
  transfers between devices with their start and end apart: 47, of which 11 were waited for; matrix products, arithmetic and copies ran while one was open for 10% of the time, Pallas kernels for 58%

commit v1 on v0

--- a/solution.py
+++ b/solution.py
@@ -89,13 +89,16 @@
 
 
 def fold(value, shifts):
-    orders = []
+    tiles = 2 * NX
+    orders, came = [], []
     for dx, dy in shifts:
-        picks = [0] * (2 * NX)
+        picks = [0] * tiles
         for n, slot in enumerate(SLOT_OF):
             picks[slot] = SLOT_OF[((n // 2 + dx) % NX) * 2 + (n % 2 + dy) % 2]
-        orders.append(tuple(picks))
-    came = [tok_shift(value, dx, dy) for dx, dy in shifts]
+        orders.append(
+            tuple(at * tiles + p for at in range(value.shape[0] // tiles) for p in picks)
+        )
+        came.append(tok_shift(value, dx, dy))
     return pl.pallas_call(
         functools.partial(fold_kernel, tuple(orders)),
         out_shape=jax.ShapeDtypeStruct(value.shape, value.dtype),
@@ -104,10 +107,12 @@
     )(value, *came)
 
 
-def sum_over_tok(value):
-    tiles = value.reshape(2 * NX, -1)
-    pair = fold(tiles, ((0, 1),))
-    return fold(pair, ((1, 0), (3, 0), (2, 0))).reshape(-1)
+def sum_over_tok(values):
+    rows = values[0].shape[0]
+    stacked = jnp.concatenate([v.reshape(2 * NX, -1) for v in values], axis=0)
+    pair = fold(stacked, ((0, 1),))
+    whole = fold(pair, ((1, 0), (3, 0), (2, 0)))
+    return [whole[n * 2 * NX : (n + 1) * 2 * NX].reshape(rows) for n in range(len(values))]
 
 
 def swap_z(value, distance):
@@ -144,99 +149,43 @@
     for bit, move in moves[::-1]:
         mine = (me >> bit) & 1
         came = move(held)
-        low, high = jnp.where(mine == 1, came, held), jnp.where(mine == 1, held, came)
         if bit:
+            low, high = jnp.where(mine == 1, came, held), jnp.where(mine == 1, held, came)
             held = jnp.concatenate([low, high], axis=0)
-    return low, high
-
-
-def gather_weights(own):
-    depth = own.shape[0]
-    beside = group_shift(own, dy=1)
-    pair = jnp.concatenate([own, beside], axis=0)
-    low, high = [pair], [pair]
-    for _ in range(1, NZ // 2):
-        low.append(group_shift(low[-1], dz=1))
-        high.append(group_shift(high[-1], dz=-1))
-    own_half, beside_half = low[-1][:depth], high[-1][depth:]
-    far_own = group_shift(own_half, dz=1)
-    far_beside = group_shift(beside_half, dz=-1)
-    me = lax.axis_index("group")
-    y, z, c = me >> 4, (me >> 1) & (NZ - 1), me & 1
-
-    def at(dy, dz, dc):
-        return ((y ^ dy) << 4) | (((z + dz) & (NZ - 1)) << 1) | (c ^ dc)
-
-    held = [(pair, ((0, 0), (1, 0)))]
-    for k in range(1, NZ // 2):
-        held.append((low[k], ((0, -k), (1, -k))))
-        held.append((high[k], ((0, k), (1, k))))
-    held.append((far_own, ((0, NZ // 2),)))
-    held.append((far_beside, ((1, NZ // 2),)))
-    pieces, places = [], []
-    for dc in range(NC):
-        for piece, where in held:
-            pieces.append(piece if dc == 0 else group_shift(piece, dc=1))
-            places += [at(dy, dz, dc) for dy, dz in where]
-    return assemble(pieces, jnp.stack(places), depth)
-
-
-def assemble_kernel(depth, places, *refs):
-    pieces, out, sem = refs[:-2], refs[-2], refs[-1]
-    copies = []
-    for piece in pieces:
-        for n in range(piece.shape[0] // depth):
-            row = pl.multiple_of(places[len(copies)] * depth, depth)
-            copies.append(
-                pltpu.make_async_copy(
-                    piece.at[pl.ds(n * depth, depth)],
-                    out.at[pl.ds(row, depth)],
-                    sem.at[len(copies)],
-                )
-            )
-    for copy in copies:
-        copy.start()
-    for copy in copies:
-        copy.wait()
-
-
-def assemble(pieces, places, depth):
-    columns = pieces[0].shape[1]
-    rows = places.shape[0] * depth
-    anywhere = pl.BlockSpec(memory_space=pl.ANY)
-    return pl.pallas_call(
-        functools.partial(assemble_kernel, depth),
-        grid_spec=pltpu.PrefetchScalarGridSpec(
-            num_scalar_prefetch=1,
-            grid=(),
-            in_specs=[anywhere] * len(pieces),
-            out_specs=anywhere,
-            scratch_shapes=[pltpu.SemaphoreType.DMA((places.shape[0],))],
-        ),
-        out_shape=jax.ShapeDtypeStruct((rows, columns), pieces[0].dtype),
-        cost_estimate=pl.CostEstimate(
-            flops=0, transcendentals=0, bytes_accessed=4 * rows * columns
-        ),
-        interpret=INTERPRET,
-        name="assemble",
-    )(places, *pieces)
+    return held, came
 
 
 def attend_kernel(
     heads, scale, order, count, slots, query, ck, cv, ek, ev, nk, nv, out, keys, values, sems
 ):
     span = ck.shape[0]
-    parts = ((ck, cv), (ek, ev), (nk, nv))
-    copies = []
-    for n, (k_part, v_part) in enumerate(parts):
-        rows = pl.ds(n * span, span)
-        copies.append(pltpu.make_async_copy(k_part, keys.at[rows], sems.at[2 * n]))
-        copies.append(pltpu.make_async_copy(v_part, values.at[rows], sems.at[2 * n + 1]))
-    for copy in copies:
+    tiles = span // TILE
+
+    def copies(parts):
+        made = []
+        for n, (part, target) in enumerate(parts):
+            rows = pl.ds((n // 2) * span, span)
+            made.append(pltpu.make_async_copy(part, target.at[rows], sems.at[n]))
+        return made
+
+    fresh = [(ek, keys), (ev, values), (nk, keys), (nv, values)]
+    straight = copies([(ck, keys), (cv, values)] + fresh)
+    crossed = copies([(cv, keys), (ck, values)] + fresh)
+
+    @pl.when(slots[tiles] == 0)
+    def _():
+        for copy in straight[:2]:
+            copy.start()
+
+    @pl.when(slots[tiles] != 0)
+    def _():
+        for copy in crossed[:2]:
+            copy.start()
+
+    for copy in straight[2:]:
         copy.start()
-    for copy in copies:
+    for copy in straight:
         copy.wait()
-    tiles = span // TILE
 
     def few_tiles(first, pairs):
         low = lax.broadcasted_iota(jnp.int32, (1, 2 * TILE), 1) < TILE
@@ -288,8 +237,9 @@
         for h in range(heads):
             for n in range(2):
                 most = jnp.maximum(most, count[h * tiles + first + n])
-        for pairs in range(2, MOST // 2 + 1):
-            pl.when(jnp.maximum((most + 1) // 2, 2) == pairs)(functools.partial(few_tiles, first, pairs))
+        few = MOST // 4
+        pl.when(most <= 2 * few)(functools.partial(few_tiles, first, few))
+        pl.when(most > 2 * few)(functools.partial(few_tiles, first, MOST // 2))
 
 
 def attend(query, parts, order, count, slots, heads):
@@ -335,7 +285,8 @@
     turn = jnp.arange(1, MOST + 1, dtype=jnp.int32)
     picked = (rank[:, :, None, :] == turn[None, None, :, None]) & (allowed[:, :, None, :] > 0)
     order = jnp.sum(jnp.where(picked, physical, 0), axis=-1)
-    return order.reshape(-1), count.reshape(-1), slots
+    core = jnp.reshape(lax.axis_index("group") & 1, (1,))
+    return order.reshape(-1), count.reshape(-1), jnp.concatenate([slots, core])
 
 
 def local(
@@ -358,23 +309,29 @@
     heads = tile_mask.shape[0]
     root = owners[owners.shape[0] - 1]
     modulated = modulate(latents, timesteps[0], mod_shift, mod_scale)
-    joined = gather_weights(jnp.concatenate([w_key, w_value, w_query], axis=1))
+    joined = lax.all_gather(
+        jnp.concatenate([w_query, w_key, w_value], axis=1), "group", axis=0, tiled=True
+    )
     tokens = jnp.concatenate(gather_tokens(modulated), axis=0)
-    cached_keys, cached_values = spread_cache(cache_keys, cache_values, root)
+    held, crossed = spread_cache(cache_keys, cache_values, root)
     order, count, slots = tile_lists(
         tile_mask, lax.axis_index("group") == 0, lax.axis_index("tok")
     )
-    both = jnp.dot(tokens, joined[:, : 2 * head_cols], preferred_element_type=jnp.float32)
-    raw_key = both[:, :head_cols]
-    value_rows = both[:, head_cols:].astype(jnp.bfloat16)
+    both = lax.optimization_barrier(
+        jnp.dot(tokens, joined[:, : 2 * head_cols], preferred_element_type=jnp.float32)
+    )
+    raw_query, raw_key = both[:, :head_cols], both[:, head_cols:]
+    query_squares, key_squares = sum_over_tok(
+        [jnp.sum(raw_query * raw_query, axis=1), jnp.sum(raw_key * raw_key, axis=1)]
+    )
+    value_rows = jnp.dot(
+        tokens, joined[:, 2 * head_cols :], preferred_element_type=jnp.float32
+    ).astype(jnp.bfloat16)
     earlier_values = from_behind(value_rows, "group", 1)
-    key_squares = sum_over_tok(jnp.sum(raw_key * raw_key, axis=1))
-    raw_query = jnp.dot(tokens, joined[:, 2 * head_cols :], preferred_element_type=jnp.float32)
     key_rows = scaled_rows(raw_key, key_squares, width, key_gain)
     earlier_keys = from_behind(key_rows, "group", 1)
-    query_squares = sum_over_tok(jnp.sum(raw_query * raw_query, axis=1))
     query_rows = scaled_rows(raw_query, query_squares, width, query_gain)
-    parts = (cached_keys, cached_values, earlier_keys, earlier_values, key_rows, value_rows)
+    parts = (held, crossed, earlier_keys, earlier_values, key_rows, value_rows)
     return attend(query_rows, parts, order, count, slots, heads)
 
 

time: 638 us -> 225 us (0.35); the launches traced: 626 us -> 222 us
  Pallas kernels: 379 us -> 16.9 us
  starting transfers between devices: 90.8 us -> 65.4 us
  waiting for transfers between devices: 82.1 us -> 66 us
  between operations: 5.19 us -> 17.6 us
  local copies, waits for them, and re-layouts: 25.3 us -> 15.1 us
    pallas_call x1 -> x0, Pallas kernels: 359 us -> none  [assemble(): pl.pallas_call(functools.partial(assemble_kernel, depth), grid_spec=pltpu...]
    ppermute x22 -> x4, waiting for transfers between devices: 42 us -> 20.7 us  [group_shift(): return lax.ppermute(value, 'group', route)]
    ppermute x22 -> x4, starting transfers between devices: 38.9 us -> 19.2 us  [group_shift(): return lax.ppermute(value, 'group', route)]
    all_gather x0 -> x1, waiting for transfers between devices: none -> 14 us  [local(): lax.all_gather(jnp.concatenate([w_query, w_key, w_value], axis=1), 'group...]
    ppermute x6, waiting for transfers between devices: 30.3 us -> 16.6 us  [swap_z(): return lax.ppermute(value, 'group', route)]
    ppermute x17 -> x13, starting transfers between devices: 23.4 us -> 15.9 us  [tok_shift(): return lax.ppermute(value, 'tok', route)]
    unnamed x82 -> x36, local copies, waits for them, and re-layouts: 16.8 us -> 12.1 us
  transfers between devices with their start and end apart: 47 -> 26, of which waited for: 11 -> 10; matrix products, arithmetic and copies ran while one was open for 10% -> 18% of each run, Pallas kernels for 58% -> 1%
where the time goes in v1:
time: 225 us; the launch traced here: 222 us
  waiting for transfers between devices  66 us (29%)
  starting transfers between devices  65.4 us (29%)
  matrix products  22.5 us (10%)
  other arithmetic  18.5 us (8%)
  between operations  17.6 us (8%)
  Pallas kernels  16.9 us (8%)
  local copies, waits for them, and re-layouts  15.1 us (7%)
    ppermute x6, starting transfers between devices, swap_z(): return lax.ppermute(value, 'group', route)  23.4 us
    ppermute x4, waiting for transfers between devices, group_shift(): return lax.ppermute(value, 'group', route)  20.7 us
    ppermute x4, starting transfers between devices, group_shift(): return lax.ppermute(value, 'group', route)  19.2 us
    ppermute x6, waiting for transfers between devices, swap_z(): return lax.ppermute(value, 'group', route)  16.6 us
    ppermute x13, starting transfers between devices, tok_shift(): return lax.ppermute(value, 'tok', route)  15.9 us
    pallas_call x1, Pallas kernels, attend(): pl.pallas_call(functools.partial(attend_kernel, heads, 1.0 / math.sqrt(wi...  14.2 us
    all_gather x1, waiting for transfers between devices, local(): lax.all_gather(jnp.concatenate([w_query, w_key, w_value], axis=1), 'group...  14 us
    dot_general x1, matrix products, local(): jnp.dot(tokens, joined[:, :2 * head_cols], preferred_element_type=jnp.flo...  12.3 us
  transfers between devices with their start and end apart: 26, of which 10 were waited for; matrix products, arithmetic and copies ran while one was open for 18% of the time, Pallas kernels for 1%

profile of v1, /device:TPU:1, one launch (start us, length us, event | category | flops | bytes accessed | tf_op | source)
XLA Modules:
  0.0 221.9 jit_solution(7539817054219242577)
XLA Ops:
  9.8 3.3 %collective-permute-start.13 = (bf16[1024,384]{1,0:T(8,128)(2,1)S(1)}, bf16[1024,384]{1,0:T(8,128)(2,1)}, u32[]{:S(2)}, u32[]{:S(2)}) collective-permute-start(bf16[1024,384]{1,0:T(8,128)(2,1)S(1)} %broadcast_select_fusion), channel_id=1, source_target_pairs={{0,8},{8,0},{16,24},{24,16},{32,40},{40,32},{48,56},{56,48},{64,72... | collective-permute-start | bytes 2359304 | tf_op jit(solution)/shard_map/ppermute | solution.py:31
  19.5 2.2 %constant_dynamic-update-slice_fusion.9 = (bf16[1024,5120]{1,0:T(8,128)(2,1)}, bf16[128,5120]{1,0:T(8,128)(2,1)}) fusion(f32[5120]{0:T(1024)S(1)} %get-tuple-element.25, f32[5120]{0:T(1024)S(1)} %copy-done.6, f32[5120]{0:T(1024)S(1)} %get-tuple-element.26, f32[128]{0:T(128)S(1)} %add_rsqrt_fusion, f32[128]{0:T(128)S(1)} %broadcast_multiply_fusion, ...), kind=kLoop, calls=%fused_computation.52 | loop fusion | flops 4587519 | bytes 3994624
  26.8 4.3 %collective-permute-done.14 = bf16[512,384]{1,0:T(8,128)(2,1)} collective-permute-done((bf16[512,384]{1,0:T(8,128)(2,1)}, bf16[512,384]{1,0:T(8,128)(2,1)}, u32[]{:S(2)}, u32[]{:S(2)}) %collective-permute-start.14) | collective-permute-done | bytes 393248 | tf_op jit(solution)/shard_map/ppermute | solution.py:31
  31.2 7.3 %collective-permute-start.15 = (bf16[256,384]{1,0:T(8,128)(2,1)S(1)}, bf16[256,384]{1,0:T(8,128)(2,1)S(1)}, u32[]{:S(2)}, u32[]{:S(2)}) collective-permute-start(bf16[256,384]{1,0:T(8,128)(2,1)S(1)} %broadcast_select_fusion.6), channel_id=1, source_target_pairs={{0,64},{8,72},{16,80},{24,88},{32,96},{40,104},{48,112},{56,120},{... | collective-permute-start | bytes 589832 | tf_op jit(solution)/shard_map/ppermute | solution.py:128
  38.5 5.2 %collective-permute-done.15 = bf16[256,384]{1,0:T(8,128)(2,1)S(1)} collective-permute-done((bf16[256,384]{1,0:T(8,128)(2,1)S(1)}, bf16[256,384]{1,0:T(8,128)(2,1)S(1)}, u32[]{:S(2)}, u32[]{:S(2)}) %collective-permute-start.15) | collective-permute-done | bytes 196640 | tf_op jit(solution)/shard_map/ppermute | solution.py:128
  43.8 8.3 %collective-permute-start.16 = (bf16[128,384]{1,0:T(8,128)(2,1)S(1)}, bf16[128,384]{1,0:T(8,128)(2,1)S(1)}, u32[]{:S(2)}, u32[]{:S(2)}) collective-permute-start(bf16[128,384]{1,0:T(8,128)(2,1)S(1)} %broadcast_select_fusion.9), channel_id=1, source_target_pairs={{0,32},{8,40},{16,48},{24,56},{32,0},{40,8},{48,16},{56,24},{64,96... | collective-permute-start | bytes 294920 | tf_op jit(solution)/shard_map/ppermute | solution.py:128
  52.6 5.2 %collective-permute-done.16 = bf16[128,384]{1,0:T(8,128)(2,1)S(1)} collective-permute-done((bf16[128,384]{1,0:T(8,128)(2,1)S(1)}, bf16[128,384]{1,0:T(8,128)(2,1)S(1)}, u32[]{:S(2)}, u32[]{:S(2)}) %collective-permute-start.16) | collective-permute-done | bytes 98336 | tf_op jit(solution)/shard_map/ppermute | solution.py:128
  59.1 3.2 %collective-permute-done.17 = bf16[64,384]{1,0:T(8,128)(2,1)S(1)} collective-permute-done((bf16[64,384]{1,0:T(8,128)(2,1)S(1)}, bf16[64,384]{1,0:T(8,128)(2,1)S(1)}, u32[]{:S(2)}, u32[]{:S(2)}) %collective-permute-start.17) | collective-permute-done | bytes 49184 | tf_op jit(solution)/shard_map/ppermute | solution.py:128
  65.5 2.7 %collective-permute-start.4 = (bf16[128,5120]{1,0:T(8,128)(2,1)}, bf16[128,5120]{1,0:T(8,128)(2,1)S(1)}, u32[]{:S(2)}, u32[]{:S(2)}) collective-permute-start(bf16[128,5120]{1,0:T(8,128)(2,1)} %collective-permute-done), channel_id=1, source_target_pairs={{0,6},{1,7},{2,0},{3,1},{4,2},{5,3},{6,4},{7,5},{8,14},{9,15},{10,... | collective-permute-start | bytes 3932168 | tf_op jit(solution)/shard_map/ppermute | solution.py:38
  68.2 2.3 %collective-permute-start.19 = (bf16[128,384]{1,0:T(8,128)(2,1)S(1)}, bf16[128,384]{1,0:T(8,128)(2,1)S(1)}, u32[]{:S(2)}, u32[]{:S(2)}) collective-permute-start(bf16[128,384]{1,0:T(8,128)(2,1)S(1)} %pad_maximum_fusion.4), channel_id=1, source_target_pairs={{0,32},{8,40},{16,48},{24,56},{32,0},{40,8},{48,16},{56,24},{64,96... | collective-permute-start | bytes 294920 | tf_op jit(solution)/shard_map/ppermute | solution.py:128
  70.5 2.5 %constant_dynamic-update-slice_fusion.8 = bf16[1024,5120]{1,0:T(8,128)(2,1)} fusion(bf16[1024,5120]{1,0:T(8,128)(2,1)} %get-tuple-element.7, bf16[128,5120]{1,0:T(8,128)(2,1)} %collective-permute-done), kind=kLoop, calls=%fused_computation.51 | loop fusion | bytes 2621440
  73.0 5.4 %collective-permute-start.20 = (bf16[256,384]{1,0:T(8,128)(2,1)S(1)}, bf16[256,384]{1,0:T(8,128)(2,1)S(1)}, u32[]{:S(2)}, u32[]{:S(2)}) collective-permute-start(bf16[256,384]{1,0:T(8,128)(2,1)S(1)} %pad_maximum_fusion.3), channel_id=1, source_target_pairs={{0,64},{8,72},{16,80},{24,88},{32,96},{40,104},{48,112},{56,120},{... | collective-permute-start | bytes 589832 | tf_op jit(solution)/shard_map/ppermute | solution.py:128
  79.6 2.9 %collective-permute-done.20 = bf16[256,384]{1,0:T(8,128)(2,1)S(1)} collective-permute-done((bf16[256,384]{1,0:T(8,128)(2,1)S(1)}, bf16[256,384]{1,0:T(8,128)(2,1)S(1)}, u32[]{:S(2)}, u32[]{:S(2)}) %collective-permute-start.20) | collective-permute-done | bytes 196640 | tf_op jit(solution)/shard_map/ppermute | solution.py:128
  82.7 14.4 %collective-permute-start.21 = (bf16[512,384]{1,0:T(8,128)(2,1)S(1)}, bf16[512,384]{1,0:T(8,128)(2,1)S(1)}, u32[]{:S(2)}, u32[]{:S(2)}) collective-permute-start(bf16[512,384]{1,0:T(8,128)(2,1)S(1)} %pad_maximum_fusion.1), channel_id=1, source_target_pairs={{0,128},{8,136},{16,144},{24,152},{32,160},{40,168},{48,176},{56,1... | collective-permute-start | bytes 1179656 | tf_op jit(solution)/shard_map/ppermute | solution.py:31
  98.2 16.4 %collective-permute-done.21 = bf16[512,384]{1,0:T(8,128)(2,1)S(1)} collective-permute-done((bf16[512,384]{1,0:T(8,128)(2,1)S(1)}, bf16[512,384]{1,0:T(8,128)(2,1)S(1)}, u32[]{:S(2)}, u32[]{:S(2)}) %collective-permute-start.21) | collective-permute-done | bytes 393248 | tf_op jit(solution)/shard_map/ppermute | solution.py:31
  115.8 2.7 %collective-permute-start.8 = (bf16[64,5120]{1,0:T(8,128)(2,1)S(1)}, bf16[64,5120]{1,0:T(8,128)(2,1)S(1)}, u32[]{:S(2)}, u32[]{:S(2)}) collective-permute-start(bf16[64,5120]{1,0:T(8,128)(2,1)S(1)} %slice.79), channel_id=1, source_target_pairs={{0,6},{1,7},{2,0},{3,1},{4,2},{5,3},{6,4},{7,5},{8,14},{9,15},{10,... | collective-permute-start | bytes 1966088 | tf_op jit(solution)/shard_map/ppermute | solution.py:38
  122.6 8.1 %collective-permute-done.7 = bf16[64,5120]{1,0:T(8,128)(2,1)S(1)} collective-permute-done((bf16[64,5120]{1,0:T(8,128)(2,1)S(1)}, bf16[64,5120]{1,0:T(8,128)(2,1)S(1)}, u32[]{:S(2)}, u32[]{:S(2)}) %collective-permute-start.7) | collective-permute-done | bytes 655392 | tf_op jit(solution)/shard_map/ppermute | solution.py:38
  132.5 14.0 %all-gather.2.cloned.1.call-done = bf16[5120,1152]{1,0:T(8,128)(2,1)} async-done(((bf16[160,1152]{1,0:T(8,128)(2,1)}), bf16[5120,1152]{1,0:T(8,128)(2,1)}) %all-gather.2.cloned.1.call-update) | async-done | bytes 11796496 | tf_op jit(solution)/shard_map/all_gather | solution.py:312
  146.5 12.3 %fusion = f32[1024,768]{1,0:T(8,128)S(1)} fusion(bf16[1024,5120]{1,0:T(8,128)(2,1)} %constant_dynamic-update-slice_fusion, bf16[5120,1152]{1,0:T(8,128)(2,1)} %all-gather.2.cloned.1.call-done), kind=kOutput, calls=%fused_computation | convolution fusion | flops 8053063680 | bytes 21495808 | tf_op jit(solution)/shard_map/dot_general | solution.py:321
  167.4 10.2 %fusion.11.nv = bf16[1024,384]{1,0:T(8,128)(2,1)} fusion(bf16[1024,5120]{1,0:T(8,128)(2,1)} %constant_dynamic-update-slice_fusion, bf16[5120,1152]{1,0:T(8,128)(2,1)} %all-gather.2.cloned.1.call-done), kind=kOutput, calls=%fused_computation.17 | convolution fusion | flops 4026925056 | bytes 15204352 | tf_op jit(solution)/shard_map/dot_general | solution.py:327
  177.6 4.7 %collective-permute-start.24 = (bf16[1024,384]{1,0:T(8,128)(2,1)}, bf16[1024,384]{1,0:T(8,128)(2,1)}, u32[]{:S(2)}, u32[]{:S(2)}) collective-permute-start(bf16[1024,384]{1,0:T(8,128)(2,1)} %fusion.11.nv), channel_id=1, source_target_pairs={{0,8},{8,16},{16,24},{24,32},{32,40},{40,48},{48,56},{56,64},{64,7... | collective-permute-start | bytes 2359304 | tf_op jit(solution)/shard_map/ppermute | solution.py:44
  187.1 2.1 collective-permute-start.23
  194.3 5.7 %collective-permute-done.23.ek = bf16[1024,384]{1,0:T(8,128)(2,1)S(1)} collective-permute-done((bf16[1024,384]{1,0:T(8,128)(2,1)}, bf16[1024,384]{1,0:T(8,128)(2,1)S(1)}, u32[]{:S(2)}, u32[]{:S(2)}) %collective-permute-start.23) | collective-permute-done | bytes 786464 | tf_op jit(solution)/shard_map/ppermute | solution.py:44
  200.8 14.2 %attend.1 = bf16[1024,384]{1,0:T(8,128)(2,1)} custom-call(s32[192]{0:T(256)} %reshape.116.order, s32[24]{0:T(128)} %reshape.117.count, s32[9]{0:T(128)} %pad_add_fusion.1.slots, bf16[1024,384]{1,0:T(8,128)(2,1)} %get-tuple-element.14.query, bf16[1024,384]{1,0:T(8,128)(2,1)} %pad_maximum_fusion.ck, bf16[1024,384]{1,0:T(8,128)(2,1)} %collective-permute-done.22.cv, ...), custom_call_target="tpu_custom_call" | custom-call | flops 1610612736 | bytes 6291456 | tf_op jit(solution)/shard_map/attend/pallas_call | solution.py:249
  (119 shorter events, 44.6 us)
Async XLA Ops:
  6.5 140.0 %all-gather.2.cloned.1.call-start = ((), (), s32[]{:S(2)}) async-start(), calls=%async_computation | async-start | bytes 12165120 | tf_op jit(solution)/shard_map/all_gather | solution.py:312
  9.8 6.2 %collective-permute-start.13 = (bf16[1024,384]{1,0:T(8,128)(2,1)S(1)}, bf16[1024,384]{1,0:T(8,128)(2,1)}, u32[]{:S(2)}, u32[]{:S(2)}) collective-permute-start(bf16[1024,384]{1,0:T(8,128)(2,1)S(1)} %broadcast_select_fusion), channel_id=1, source_target_pairs={{0,8},{8,0},{16,24},{24,16},{32,40},{40,32},{48,56},{56,48},{64,72... | collective-permute-start | bytes 2359304 | tf_op jit(solution)/shard_map/ppermute | solution.py:31
  18.3 12.8 %collective-permute-start.14 = (bf16[512,384]{1,0:T(8,128)(2,1)}, bf16[512,384]{1,0:T(8,128)(2,1)}, u32[]{:S(2)}, u32[]{:S(2)}) collective-permute-start(bf16[512,384]{1,0:T(8,128)(2,1)} %broadcast_select_fusion.3), channel_id=1, source_target_pairs={{0,128},{8,136},{16,144},{24,152},{32,160},{40,168},{48,176},{56,1... | collective-permute-start | bytes 1179656 | tf_op jit(solution)/shard_map/ppermute | solution.py:31
  21.8 43.7 %collective-permute-start = (bf16[128,5120]{1,0:T(8,128)(2,1)}, bf16[128,5120]{1,0:T(8,128)(2,1)}, u32[]{:S(2)}, u32[]{:S(2)}) collective-permute-start(bf16[128,5120]{1,0:T(8,128)(2,1)} %get-tuple-element.8), channel_id=1, source_target_pairs={{0,1},{1,0},{2,3},{3,2},{4,5},{5,4},{6,7},{7,6},{8,9},{9,8},{10,11... | collective-permute-start | bytes 3932168 | tf_op jit(solution)/shard_map/ppermute | solution.py:38
  22.2 40.4 %collective-permute-start.1 = (bf16[128,5120]{1,0:T(8,128)(2,1)}, bf16[128,5120]{1,0:T(8,128)(2,1)S(1)}, u32[]{:S(2)}, u32[]{:S(2)}) collective-permute-start(bf16[128,5120]{1,0:T(8,128)(2,1)} %get-tuple-element.8), channel_id=1, source_target_pairs={{0,2},{1,3},{2,4},{3,5},{4,6},{5,7},{6,0},{7,1},{8,10},{9,11},{10,... | collective-permute-start | bytes 3932168 | tf_op jit(solution)/shard_map/ppermute | solution.py:38
  23.4 40.1 %collective-permute-start.2 = (bf16[128,5120]{1,0:T(8,128)(2,1)}, bf16[128,5120]{1,0:T(8,128)(2,1)S(1)}, u32[]{:S(2)}, u32[]{:S(2)}) collective-permute-start(bf16[128,5120]{1,0:T(8,128)(2,1)} %get-tuple-element.8), channel_id=1, source_target_pairs={{0,6},{1,7},{2,0},{3,1},{4,2},{5,3},{6,4},{7,5},{8,14},{9,15},{10,... | collective-permute-start | bytes 3932168 | tf_op jit(solution)/shard_map/ppermute | solution.py:38
  31.2 12.4 %collective-permute-start.15 = (bf16[256,384]{1,0:T(8,128)(2,1)S(1)}, bf16[256,384]{1,0:T(8,128)(2,1)S(1)}, u32[]{:S(2)}, u32[]{:S(2)}) collective-permute-start(bf16[256,384]{1,0:T(8,128)(2,1)S(1)} %broadcast_select_fusion.6), channel_id=1, source_target_pairs={{0,64},{8,72},{16,80},{24,88},{32,96},{40,104},{48,112},{56,120},{... | collective-permute-start | bytes 589832 | tf_op jit(solution)/shard_map/ppermute | solution.py:128
  43.8 14.0 %collective-permute-start.16 = (bf16[128,384]{1,0:T(8,128)(2,1)S(1)}, bf16[128,384]{1,0:T(8,128)(2,1)S(1)}, u32[]{:S(2)}, u32[]{:S(2)}) collective-permute-start(bf16[128,384]{1,0:T(8,128)(2,1)S(1)} %broadcast_select_fusion.9), channel_id=1, source_target_pairs={{0,32},{8,40},{16,48},{24,56},{32,0},{40,8},{48,16},{56,24},{64,96... | collective-permute-start | bytes 294920 | tf_op jit(solution)/shard_map/ppermute | solution.py:128
  62.4 5.8 %collective-permute-start.18 = (bf16[64,384]{1,0:T(8,128)(2,1)S(1)}, bf16[64,384]{1,0:T(8,128)(2,1)S(1)}, u32[]{:S(2)}, u32[]{:S(2)}) collective-permute-start(bf16[64,384]{1,0:T(8,128)(2,1)S(1)} %select_select_fusion.4), channel_id=1, source_target_pairs={{0,16},{8,24},{16,0},{24,8},{32,48},{40,56},{48,32},{56,40},{64,80... | collective-permute-start | bytes 147464 | tf_op jit(solution)/shard_map/ppermute | solution.py:128
  62.6 58.2 %collective-permute-start.5 = (bf16[64,5120]{1,0:T(8,128)(2,1)S(1)}, bf16[64,5120]{1,0:T(8,128)(2,1)S(1)}, u32[]{:S(2)}, u32[]{:S(2)}) collective-permute-start(bf16[64,5120]{1,0:T(8,128)(2,1)S(1)} %slice.76), channel_id=1, source_target_pairs={{0,2},{1,3},{2,4},{3,5},{4,6},{5,7},{6,0},{7,1},{8,10},{9,11},{10,... | collective-permute-start | bytes 1966088 | tf_op jit(solution)/shard_map/ppermute | solution.py:38
  63.5 58.2 %collective-permute-start.6 = (bf16[64,5120]{1,0:T(8,128)(2,1)S(1)}, bf16[64,5120]{1,0:T(8,128)(2,1)S(1)}, u32[]{:S(2)}, u32[]{:S(2)}) collective-permute-start(bf16[64,5120]{1,0:T(8,128)(2,1)S(1)} %slice.77), channel_id=1, source_target_pairs={{0,6},{1,7},{2,0},{3,1},{4,2},{5,3},{6,4},{7,5},{8,14},{9,15},{10,... | collective-permute-start | bytes 1966088 | tf_op jit(solution)/shard_map/ppermute | solution.py:38
  65.5 50.1 %collective-permute-start.3 = (bf16[128,5120]{1,0:T(8,128)(2,1)}, bf16[128,5120]{1,0:T(8,128)(2,1)S(1)}, u32[]{:S(2)}, u32[]{:S(2)}) collective-permute-start(bf16[128,5120]{1,0:T(8,128)(2,1)} %collective-permute-done), channel_id=1, source_target_pairs={{0,2},{1,3},{2,4},{3,5},{4,6},{5,7},{6,0},{7,1},{8,10},{9,11},{10,... | collective-permute-start | bytes 3932168 | tf_op jit(solution)/shard_map/ppermute | solution.py:38
  65.5 50.2 %collective-permute-start.4 = (bf16[128,5120]{1,0:T(8,128)(2,1)}, bf16[128,5120]{1,0:T(8,128)(2,1)S(1)}, u32[]{:S(2)}, u32[]{:S(2)}) collective-permute-start(bf16[128,5120]{1,0:T(8,128)(2,1)} %collective-permute-done), channel_id=1, source_target_pairs={{0,6},{1,7},{2,0},{3,1},{4,2},{5,3},{6,4},{7,5},{8,14},{9,15},{10,... | collective-permute-start | bytes 3932168 | tf_op jit(solution)/shard_map/ppermute | solution.py:38
  68.2 4.7 %collective-permute-start.19 = (bf16[128,384]{1,0:T(8,128)(2,1)S(1)}, bf16[128,384]{1,0:T(8,128)(2,1)S(1)}, u32[]{:S(2)}, u32[]{:S(2)}) collective-permute-start(bf16[128,384]{1,0:T(8,128)(2,1)S(1)} %pad_maximum_fusion.4), channel_id=1, source_target_pairs={{0,32},{8,40},{16,48},{24,56},{32,0},{40,8},{48,16},{56,24},{64,96... | collective-permute-start | bytes 294920 | tf_op jit(solution)/shard_map/ppermute | solution.py:128
  73.0 9.5 %collective-permute-start.20 = (bf16[256,384]{1,0:T(8,128)(2,1)S(1)}, bf16[256,384]{1,0:T(8,128)(2,1)S(1)}, u32[]{:S(2)}, u32[]{:S(2)}) collective-permute-start(bf16[256,384]{1,0:T(8,128)(2,1)S(1)} %pad_maximum_fusion.3), channel_id=1, source_target_pairs={{0,64},{8,72},{16,80},{24,88},{32,96},{40,104},{48,112},{56,120},{... | collective-permute-start | bytes 589832 | tf_op jit(solution)/shard_map/ppermute | solution.py:128
  82.7 32.0 %collective-permute-start.21 = (bf16[512,384]{1,0:T(8,128)(2,1)S(1)}, bf16[512,384]{1,0:T(8,128)(2,1)S(1)}, u32[]{:S(2)}, u32[]{:S(2)}) collective-permute-start(bf16[512,384]{1,0:T(8,128)(2,1)S(1)} %pad_maximum_fusion.1), channel_id=1, source_target_pairs={{0,128},{8,136},{16,144},{24,152},{32,160},{40,168},{48,176},{56,1... | collective-permute-start | bytes 1179656 | tf_op jit(solution)/shard_map/ppermute | solution.py:31
  115.6 15.1 %collective-permute-start.7 = (bf16[64,5120]{1,0:T(8,128)(2,1)S(1)}, bf16[64,5120]{1,0:T(8,128)(2,1)S(1)}, u32[]{:S(2)}, u32[]{:S(2)}) collective-permute-start(bf16[64,5120]{1,0:T(8,128)(2,1)S(1)} %slice.78), channel_id=1, source_target_pairs={{0,2},{1,3},{2,4},{3,5},{4,6},{5,7},{6,0},{7,1},{8,10},{9,11},{10,... | collective-permute-start | bytes 1966088 | tf_op jit(solution)/shard_map/ppermute | solution.py:38
  115.8 15.8 %collective-permute-start.8 = (bf16[64,5120]{1,0:T(8,128)(2,1)S(1)}, bf16[64,5120]{1,0:T(8,128)(2,1)S(1)}, u32[]{:S(2)}, u32[]{:S(2)}) collective-permute-start(bf16[64,5120]{1,0:T(8,128)(2,1)S(1)} %slice.79), channel_id=1, source_target_pairs={{0,6},{1,7},{2,0},{3,1},{4,2},{5,3},{6,4},{7,5},{8,14},{9,15},{10,... | collective-permute-start | bytes 1966088 | tf_op jit(solution)/shard_map/ppermute | solution.py:38
  160.8 33.5 %collective-permute-start.22 = (bf16[1024,384]{1,0:T(8,128)(2,1)}, bf16[1024,384]{1,0:T(8,128)(2,1)}, u32[]{:S(2)}, u32[]{:S(2)}) collective-permute-start(bf16[1024,384]{1,0:T(8,128)(2,1)} %pad_maximum_fusion.ck), channel_id=1, source_target_pairs={{0,8},{8,0},{16,24},{24,16},{32,40},{40,32},{48,56},{56,48},{64,72... | collective-permute-start | bytes 2359304 | tf_op jit(solution)/shard_map/ppermute | solution.py:31
  163.2 19.1 %collective-permute-start.10 = (f32[16,128]{1,0:T(8,128)}, f32[16,128]{1,0:T(8,128)S(1)}, u32[]{:S(2)}, u32[]{:S(2)}) collective-permute-start(f32[16,128]{1,0:T(8,128)} %fold.2.held), channel_id=1, source_target_pairs={{0,2},{1,3},{2,4},{3,5},{4,6},{5,7},{6,0},{7,1},{8,10},{9,11},{10,... | collective-permute-start | bytes 24584 | tf_op jit(solution)/shard_map/ppermute | solution.py:38
  164.4 17.9 %collective-permute-start.11 = (f32[16,128]{1,0:T(8,128)}, f32[16,128]{1,0:T(8,128)S(1)}, u32[]{:S(2)}, u32[]{:S(2)}) collective-permute-start(f32[16,128]{1,0:T(8,128)} %fold.2.held), channel_id=1, source_target_pairs={{0,6},{1,7},{2,0},{3,1},{4,2},{5,3},{6,4},{7,5},{8,14},{9,15},{10,... | collective-permute-start | bytes 24584 | tf_op jit(solution)/shard_map/ppermute | solution.py:38
  165.9 16.5 %collective-permute-start.12 = (f32[16,128]{1,0:T(8,128)}, f32[16,128]{1,0:T(8,128)S(1)}, u32[]{:S(2)}, u32[]{:S(2)}) collective-permute-start(f32[16,128]{1,0:T(8,128)} %fold.2.held), channel_id=1, source_target_pairs={{0,4},{1,5},{2,6},{3,7},{4,0},{5,1},{6,2},{7,3},{8,12},{9,13},{10,... | collective-permute-start | bytes 24584 | tf_op jit(solution)/shard_map/ppermute | solution.py:38
  177.6 16.7 %collective-permute-start.24 = (bf16[1024,384]{1,0:T(8,128)(2,1)}, bf16[1024,384]{1,0:T(8,128)(2,1)}, u32[]{:S(2)}, u32[]{:S(2)}) collective-permute-start(bf16[1024,384]{1,0:T(8,128)(2,1)} %fusion.11.nv), channel_id=1, source_target_pairs={{0,8},{8,16},{16,24},{24,32},{32,40},{40,48},{48,56},{56,64},{64,7... | collective-permute-start | bytes 2359304 | tf_op jit(solution)/shard_map/ppermute | solution.py:44
  187.1 12.8 %collective-permute-start.23 = (bf16[1024,384]{1,0:T(8,128)(2,1)}, bf16[1024,384]{1,0:T(8,128)(2,1)S(1)}, u32[]{:S(2)}, u32[]{:S(2)}) collective-permute-start(bf16[1024,384]{1,0:T(8,128)(2,1)} %get-tuple-element.13.nk), channel_id=1, source_target_pairs={{0,8},{8,16},{16,24},{24,32},{32,40},{40,48},{48,56},{56,64},{64,7... | collective-permute-start | bytes 2359304 | tf_op jit(solution)/shard_map/ppermute | solution.py:44
  (16 other events, 123.2 us)
Sparse Core Ops, SparseCore 0:
  10.1 136.3 all-gather.1

commit v2 on v1

--- a/solution.py
+++ b/solution.py
@@ -133,9 +133,9 @@
     moves = (
         (0, lambda v: group_shift(v, dc=1)),
         (4, lambda v: group_shift(v, dy=1)),
+        (1, lambda v: swap_z(v, 1)),
+        (2, lambda v: swap_z(v, 2)),
         (3, lambda v: swap_z(v, 4)),
-        (2, lambda v: swap_z(v, 2)),
-        (1, lambda v: swap_z(v, 1)),
     )
     low, high = cache_keys, cache_values
     for bit, move in moves:
@@ -233,13 +233,7 @@
     @pl.loop(0, tiles // 2)
     def _(step):
         first = 2 * step
-        most = count[first]
-        for h in range(heads):
-            for n in range(2):
-                most = jnp.maximum(most, count[h * tiles + first + n])
-        few = MOST // 4
-        pl.when(most <= 2 * few)(functools.partial(few_tiles, first, few))
-        pl.when(most > 2 * few)(functools.partial(few_tiles, first, MOST // 2))
+        few_tiles(first, MOST // 2)
 
 
 def attend(query, parts, order, count, slots, heads):
@@ -309,24 +303,41 @@
     heads = tile_mask.shape[0]
     root = owners[owners.shape[0] - 1]
     modulated = modulate(latents, timesteps[0], mod_shift, mod_scale)
-    joined = lax.all_gather(
-        jnp.concatenate([w_query, w_key, w_value], axis=1), "group", axis=0, tiled=True
-    )
+    own_w = jnp.concatenate([w_query, w_key, w_value], axis=1)
+    beside_w = group_shift(own_w, dy=1)
+    planes = [[y * NZ * NC + n for n in range(NZ * NC)] for y in range(NY)]
+    weights = []
+    for w in (own_w, beside_w):
+        weights.append(
+            lax.all_gather(w, "group", axis_index_groups=planes, axis=0, tiled=True)
+        )
+    depth = weights[0].shape[0]
+    modulated = modulate(latents, timesteps[0], mod_shift, mod_scale)
+    swapped = jnp.concatenate([modulated[:, depth:], modulated[:, :depth]], axis=1)
+    modulated = jnp.where(lax.axis_index("group") < NZ * NC, modulated, swapped)
     tokens = jnp.concatenate(gather_tokens(modulated), axis=0)
+
+    def projected(first, last):
+        parts = [
+            jnp.dot(
+                tokens[:, n * depth : (n + 1) * depth],
+                w[:, first:last],
+                preferred_element_type=jnp.float32,
+            )
+            for n, w in enumerate(weights)
+        ]
+        return parts[0] + parts[1]
+
     held, crossed = spread_cache(cache_keys, cache_values, root)
     order, count, slots = tile_lists(
         tile_mask, lax.axis_index("group") == 0, lax.axis_index("tok")
     )
-    both = lax.optimization_barrier(
-        jnp.dot(tokens, joined[:, : 2 * head_cols], preferred_element_type=jnp.float32)
-    )
+    both = lax.optimization_barrier(projected(0, 2 * head_cols))
     raw_query, raw_key = both[:, :head_cols], both[:, head_cols:]
     query_squares, key_squares = sum_over_tok(
         [jnp.sum(raw_query * raw_query, axis=1), jnp.sum(raw_key * raw_key, axis=1)]
     )
-    value_rows = jnp.dot(
-        tokens, joined[:, 2 * head_cols :], preferred_element_type=jnp.float32
-    ).astype(jnp.bfloat16)
+    value_rows = projected(2 * head_cols, 3 * head_cols).astype(jnp.bfloat16)
     earlier_values = from_behind(value_rows, "group", 1)
     key_rows = scaled_rows(raw_key, key_squares, width, key_gain)
     earlier_keys = from_behind(key_rows, "group", 1)

time: 225 us -> 232 us (1.031)
  the two profiles are of different devices: /device:TPU:1 before, /device:TPU:28 now
where the time goes in v2:
time: 232 us; the launch traced here: 231 us
  waiting for transfers between devices  90.2 us (39%)
  starting transfers between devices  40.7 us (18%)
  matrix products  31.4 us (14%)
  local copies, waits for them, and re-layouts  20.3 us (9%)
  between operations  17.3 us (7%)
  Pallas kernels  16.8 us (7%)
  other arithmetic  14.1 us (6%)
    ppermute x6, waiting for transfers between devices, swap_z(): return lax.ppermute(value, 'group', route)  32.8 us
    dot_general x4, matrix products, projected(): jnp.dot(tokens[:, n * depth:(n + 1) * depth], w[:, first:last], preferred...  31.4 us
    ppermute x5, waiting for transfers between devices, group_shift(): return lax.ppermute(value, 'group', route)  23.9 us
    ppermute x13, waiting for transfers between devices, tok_shift(): return lax.ppermute(value, 'tok', route)  19.1 us
    ppermute x6, starting transfers between devices, swap_z(): return lax.ppermute(value, 'group', route)  17.3 us
    unnamed x46, local copies, waits for them, and re-layouts  16.3 us
    ppermute x13, starting transfers between devices, tok_shift(): return lax.ppermute(value, 'tok', route)  16.2 us
    pallas_call x1, Pallas kernels, attend(): pl.pallas_call(functools.partial(attend_kernel, heads, 1.0 / math.sqrt(wi...  14.1 us
  transfers between devices with their start and end apart: 28, of which 13 were waited for; matrix products, arithmetic and copies ran while one was open for 25% of the time, Pallas kernels for 1%

profile of v2, /device:TPU:28, one launch (start us, length us, event | category | flops | bytes accessed | tf_op | source)
XLA Modules:
  0.0 230.9 jit_solution(16284849227513668994)
XLA Ops:
  10.7 10.6 %collective-permute-done.9 = bf16[160,1152]{1,0:T(8,128)(2,1)S(1)} collective-permute-done((bf16[160,1152]{1,0:T(8,128)(2,1)S(1)}, bf16[160,1152]{1,0:T(8,128)(2,1)S(1)}, u32[]{:S(2)}, u32[]{:S(2)}) %collective-permute-start.9) | collective-permute-done | bytes 368672 | tf_op jit(solution)/shard_map/ppermute | solution.py:31
  31.8 2.4 %constant_dynamic-update-slice_fusion.9 = (bf16[1024,5120]{1,0:T(8,128)(2,1)}, bf16[128,5120]{1,0:T(8,128)(2,1)}) fusion(bf16[128,2560]{1,0:T(8,128)(2,1)S(1)} %get-tuple-element.16, bf16[128,2560]{1,0:T(8,128)(2,1)S(1)} %get-tuple-element.15, pred[]{:T(512)S(6)} %lt.11, f32[5120]{0:T(1024)S(1)} %get-tuple-element.27, f32[5120]{0:T(1024)S(1)} %copy-done.7, ...), kind=kLoop, calls=%fused_computation.61 | loop fusion | flops 7864319 | bytes 5305345
  38.0 5.7 %collective-permute-done.15 = bf16[512,384]{1,0:T(8,128)(2,1)} collective-permute-done((bf16[512,384]{1,0:T(8,128)(2,1)}, bf16[512,384]{1,0:T(8,128)(2,1)}, u32[]{:S(2)}, u32[]{:S(2)}) %collective-permute-start.15) | collective-permute-done | bytes 393248 | tf_op jit(solution)/shard_map/ppermute | solution.py:31
  46.8 10.1 %collective-permute-done.16 = bf16[256,384]{1,0:T(8,128)(2,1)S(1)} collective-permute-done((bf16[256,384]{1,0:T(8,128)(2,1)S(1)}, bf16[256,384]{1,0:T(8,128)(2,1)S(1)}, u32[]{:S(2)}, u32[]{:S(2)}) %collective-permute-start.16) | collective-permute-done | bytes 196640 | tf_op jit(solution)/shard_map/ppermute | solution.py:128
  57.0 3.0 %collective-permute-start.17 = (bf16[128,384]{1,0:T(8,128)(2,1)S(1)}, bf16[128,384]{1,0:T(8,128)(2,1)S(1)}, u32[]{:S(2)}, u32[]{:S(2)}) collective-permute-start(bf16[128,384]{1,0:T(8,128)(2,1)S(1)} %broadcast_select_fusion.9), channel_id=1, source_target_pairs={{0,32},{8,40},{16,48},{24,56},{32,0},{40,8},{48,16},{56,24},{64,96... | collective-permute-start | bytes 294920 | tf_op jit(solution)/shard_map/ppermute | solution.py:128
  60.0 7.4 %collective-permute-done.17 = bf16[128,384]{1,0:T(8,128)(2,1)S(1)} collective-permute-done((bf16[128,384]{1,0:T(8,128)(2,1)S(1)}, bf16[128,384]{1,0:T(8,128)(2,1)S(1)}, u32[]{:S(2)}, u32[]{:S(2)}) %collective-permute-start.17) | collective-permute-done | bytes 98336 | tf_op jit(solution)/shard_map/ppermute | solution.py:128
  67.4 6.9 %collective-permute-start.18 = (bf16[64,384]{1,0:T(8,128)(2,1)S(1)}, bf16[64,384]{1,0:T(8,128)(2,1)S(1)}, u32[]{:S(2)}, u32[]{:S(2)}) collective-permute-start(bf16[64,384]{1,0:T(8,128)(2,1)S(1)} %broadcast_select_fusion.12), channel_id=1, source_target_pairs={{0,64},{8,72},{16,80},{24,88},{32,96},{40,104},{48,112},{56,120},{... | collective-permute-start | bytes 147464 | tf_op jit(solution)/shard_map/ppermute | solution.py:128
  74.9 2.3 collective-permute-done.18
  77.2 5.2 %collective-permute-start.19 = (bf16[64,384]{1,0:T(8,128)(2,1)S(1)}, bf16[64,384]{1,0:T(8,128)(2,1)S(1)}, u32[]{:S(2)}, u32[]{:S(2)}) collective-permute-start(bf16[64,384]{1,0:T(8,128)(2,1)S(1)} %select_select_fusion.4), channel_id=1, source_target_pairs={{0,64},{8,72},{16,80},{24,88},{32,96},{40,104},{48,112},{56,120},{... | collective-permute-start | bytes 147464 | tf_op jit(solution)/shard_map/ppermute | solution.py:128
  87.0 2.5 %constant_dynamic-update-slice_fusion.8 = bf16[1024,5120]{1,0:T(8,128)(2,1)} fusion(bf16[1024,5120]{1,0:T(8,128)(2,1)} %get-tuple-element.7, bf16[128,5120]{1,0:T(8,128)(2,1)} %collective-permute-done), kind=kLoop, calls=%fused_computation.60 | loop fusion | bytes 2621440
  89.5 3.7 %collective-permute-done.20 = bf16[128,384]{1,0:T(8,128)(2,1)S(1)} collective-permute-done((bf16[128,384]{1,0:T(8,128)(2,1)S(1)}, bf16[128,384]{1,0:T(8,128)(2,1)S(1)}, u32[]{:S(2)}, u32[]{:S(2)}) %collective-permute-start.20) | collective-permute-done | bytes 98336 | tf_op jit(solution)/shard_map/ppermute | solution.py:128
  94.5 9.3 %collective-permute-done.21 = bf16[256,384]{1,0:T(8,128)(2,1)S(1)} collective-permute-done((bf16[256,384]{1,0:T(8,128)(2,1)S(1)}, bf16[256,384]{1,0:T(8,128)(2,1)S(1)}, u32[]{:S(2)}, u32[]{:S(2)}) %collective-permute-start.21) | collective-permute-done | bytes 196640 | tf_op jit(solution)/shard_map/ppermute | solution.py:128
  105.7 7.6 %collective-permute-done.22 = bf16[512,384]{1,0:T(8,128)(2,1)S(1)} collective-permute-done((bf16[512,384]{1,0:T(8,128)(2,1)S(1)}, bf16[512,384]{1,0:T(8,128)(2,1)S(1)}, u32[]{:S(2)}, u32[]{:S(2)}) %collective-permute-start.22) | collective-permute-done | bytes 393248 | tf_op jit(solution)/shard_map/ppermute | solution.py:31
  114.4 11.2 %collective-permute-done.3 = bf16[128,5120]{1,0:T(8,128)(2,1)S(1)} collective-permute-done((bf16[128,5120]{1,0:T(8,128)(2,1)}, bf16[128,5120]{1,0:T(8,128)(2,1)S(1)}, u32[]{:S(2)}, u32[]{:S(2)}) %collective-permute-start.3) | collective-permute-done | bytes 1310752 | tf_op jit(solution)/shard_map/ppermute | solution.py:38
  132.1 7.8 %collective-permute-done.7 = bf16[64,5120]{1,0:T(8,128)(2,1)S(1)} collective-permute-done((bf16[64,5120]{1,0:T(8,128)(2,1)S(1)}, bf16[64,5120]{1,0:T(8,128)(2,1)S(1)}, u32[]{:S(2)}, u32[]{:S(2)}) %collective-permute-start.7) | collective-permute-done | bytes 655392 | tf_op jit(solution)/shard_map/ppermute | solution.py:38
  141.8 9.6 %fusion.2 = f32[1024,768]{1,0:T(8,128)} fusion(bf16[1024,5120]{1,0:T(8,128)(2,1)} %constant_dynamic-update-slice_fusion, bf16[2560,1152]{1,0:T(8,128)(2,1)} %all-gather.5.cloned.1.call-done), kind=kOutput, calls=%fused_computation.2 | convolution fusion | flops 4026531840 | bytes 12320768 | tf_op jit(solution)/shard_map/dot_general | solution.py:322
  151.4 8.9 %fusion.19 = f32[1024,768]{1,0:T(8,128)S(1)} fusion(f32[1024,768]{1,0:T(8,128)} %fusion.2, bf16[2560,1152]{1,0:T(8,128)(2,1)} %all-gather.3.cloned.1.call-done, bf16[1024,5120]{1,0:T(8,128)(2,1)} %constant_dynamic-update-slice_fusion), kind=kOutput, calls=%fused_computation.21 | convolution fusion | flops 4027318272 | bytes 15466496 | tf_op jit(solution)/shard_map/dot_general | solution.py:322
  162.8 5.6 %fusion = f32[1024,384]{1,0:T(8,128)} fusion(bf16[1024,5120]{1,0:T(8,128)(2,1)S(1)} %copy-done.6, bf16[2560,1152]{1,0:T(8,128)(2,1)} %all-gather.5.cloned.1.call-done), kind=kOutput, calls=%fused_computation | convolution fusion | flops 2013265920 | bytes 8781824 | tf_op jit(solution)/shard_map/dot_general | solution.py:322
  170.3 2.7 %collective-permute-start.11 = (f32[16,128]{1,0:T(8,128)}, f32[16,128]{1,0:T(8,128)S(1)}, u32[]{:S(2)}, u32[]{:S(2)}) collective-permute-start(f32[16,128]{1,0:T(8,128)} %fold.2.held), channel_id=1, source_target_pairs={{0,2},{1,3},{2,4},{3,5},{4,6},{5,7},{6,0},{7,1},{8,10},{9,11},{10,... | collective-permute-start | bytes 24584 | tf_op jit(solution)/shard_map/ppermute | solution.py:38
  172.9 3.1 %collective-permute-start.13 = (f32[16,128]{1,0:T(8,128)}, f32[16,128]{1,0:T(8,128)S(1)}, u32[]{:S(2)}, u32[]{:S(2)}) collective-permute-start(f32[16,128]{1,0:T(8,128)} %fold.2.held), channel_id=1, source_target_pairs={{0,4},{1,5},{2,6},{3,7},{4,0},{5,1},{6,2},{7,3},{8,12},{9,13},{10,... | collective-permute-start | bytes 24584 | tf_op jit(solution)/shard_map/ppermute | solution.py:38
  176.0 7.3 %add_convert_fusion.nv = bf16[1024,384]{1,0:T(8,128)(2,1)} fusion(f32[1024,384]{1,0:T(8,128)} %fusion, bf16[2560,1152]{1,0:T(8,128)(2,1)} %all-gather.3.cloned.1.call-done, bf16[1024,5120]{1,0:T(8,128)(2,1)} %constant_dynamic-update-slice_fusion), kind=kOutput, calls=%fused_computation.22 | convolution fusion | flops 2014052352 | bytes 9568256 | tf_op jit(solution)/shard_map/dot_general | solution.py:322
  195.3 5.4 %collective-permute-done.25.ev = bf16[1024,384]{1,0:T(8,128)(2,1)} collective-permute-done((bf16[1024,384]{1,0:T(8,128)(2,1)}, bf16[1024,384]{1,0:T(8,128)(2,1)}, u32[]{:S(2)}, u32[]{:S(2)}) %collective-permute-start.25) | collective-permute-done | bytes 786464 | tf_op jit(solution)/shard_map/ppermute | solution.py:44
  200.7 8.3 %collective-permute-done.24.ek = bf16[1024,384]{1,0:T(8,128)(2,1)S(1)} collective-permute-done((bf16[1024,384]{1,0:T(8,128)(2,1)}, bf16[1024,384]{1,0:T(8,128)(2,1)S(1)}, u32[]{:S(2)}, u32[]{:S(2)}) %collective-permute-start.24) | collective-permute-done | bytes 786464 | tf_op jit(solution)/shard_map/ppermute | solution.py:44
  209.9 14.1 %attend.1 = bf16[1024,384]{1,0:T(8,128)(2,1)} custom-call(s32[192]{0:T(256)} %reshape.116.order, s32[24]{0:T(128)} %reshape.117.count, s32[9]{0:T(128)} %pad_add_fusion.1.slots, bf16[1024,384]{1,0:T(8,128)(2,1)} %get-tuple-element.14.query, bf16[1024,384]{1,0:T(8,128)(2,1)} %pad_maximum_fusion.ck, bf16[1024,384]{1,0:T(8,128)(2,1)} %collective-permute-done.23.cv, ...), custom_call_target="tpu_custom_call" | custom-call | flops 1610612736 | bytes 6291456 | tf_op jit(solution)/shard_map/attend/pallas_call | solution.py:243
  (138 shorter events, 52.8 us)
Async XLA Ops:
  6.5 135.3 %all-gather.5.cloned.1.call-start = ((), (), s32[]{:S(2)}) async-start(), calls=%async_computation.1 | async-start | bytes 6266880 | tf_op jit(solution)/shard_map/all_gather | solution.py:312
  9.4 11.9 %collective-permute-start.9 = (bf16[160,1152]{1,0:T(8,128)(2,1)S(1)}, bf16[160,1152]{1,0:T(8,128)(2,1)S(1)}, u32[]{:S(2)}, u32[]{:S(2)}) collective-permute-start(bf16[160,1152]{1,0:T(8,128)(2,1)S(1)} %constant_dynamic-update-slice_fusion.10), channel_id=1, source_target_pairs={{0,128},{8,136},{16,144},{24,152},{32,160},{40,168},{48,176},{56,1... | collective-permute-start | bytes 1105928 | tf_op jit(solution)/shard_map/ppermute | solution.py:31
  22.1 129.3 %all-gather.3.cloned.1.call-start = ((), (), s32[]{:S(2)}) async-start(), calls=%async_computation | async-start | bytes 6266880 | tf_op jit(solution)/shard_map/all_gather | solution.py:312
  30.5 13.1 %collective-permute-start.15 = (bf16[512,384]{1,0:T(8,128)(2,1)}, bf16[512,384]{1,0:T(8,128)(2,1)}, u32[]{:S(2)}, u32[]{:S(2)}) collective-permute-start(bf16[512,384]{1,0:T(8,128)(2,1)} %broadcast_select_fusion.3), channel_id=1, source_target_pairs={{0,128},{8,136},{16,144},{24,152},{32,160},{40,168},{48,176},{56,1... | collective-permute-start | bytes 1179656 | tf_op jit(solution)/shard_map/ppermute | solution.py:31
  34.2 50.6 %collective-permute-start = (bf16[128,5120]{1,0:T(8,128)(2,1)}, bf16[128,5120]{1,0:T(8,128)(2,1)}, u32[]{:S(2)}, u32[]{:S(2)}) collective-permute-start(bf16[128,5120]{1,0:T(8,128)(2,1)} %get-tuple-element.8), channel_id=1, source_target_pairs={{0,1},{1,0},{2,3},{3,2},{4,5},{5,4},{6,7},{7,6},{8,9},{9,8},{10,11... | collective-permute-start | bytes 3932168 | tf_op jit(solution)/shard_map/ppermute | solution.py:38
  34.2 48.3 %collective-permute-start.1 = (bf16[128,5120]{1,0:T(8,128)(2,1)}, bf16[128,5120]{1,0:T(8,128)(2,1)S(1)}, u32[]{:S(2)}, u32[]{:S(2)}) collective-permute-start(bf16[128,5120]{1,0:T(8,128)(2,1)} %get-tuple-element.8), channel_id=1, source_target_pairs={{0,2},{1,3},{2,4},{3,5},{4,6},{5,7},{6,0},{7,1},{8,10},{9,11},{10,... | collective-permute-start | bytes 3932168 | tf_op jit(solution)/shard_map/ppermute | solution.py:38
  35.4 48.5 %collective-permute-start.2 = (bf16[128,5120]{1,0:T(8,128)(2,1)}, bf16[128,5120]{1,0:T(8,128)(2,1)S(1)}, u32[]{:S(2)}, u32[]{:S(2)}) collective-permute-start(bf16[128,5120]{1,0:T(8,128)(2,1)} %get-tuple-element.8), channel_id=1, source_target_pairs={{0,6},{1,7},{2,0},{3,1},{4,2},{5,3},{6,4},{7,5},{8,14},{9,15},{10,... | collective-permute-start | bytes 3932168 | tf_op jit(solution)/shard_map/ppermute | solution.py:38
  44.8 12.1 %collective-permute-start.16 = (bf16[256,384]{1,0:T(8,128)(2,1)S(1)}, bf16[256,384]{1,0:T(8,128)(2,1)S(1)}, u32[]{:S(2)}, u32[]{:S(2)}) collective-permute-start(bf16[256,384]{1,0:T(8,128)(2,1)S(1)} %broadcast_select_fusion.6), channel_id=1, source_target_pairs={{0,16},{8,24},{16,0},{24,8},{32,48},{40,56},{48,32},{56,40},{64,80... | collective-permute-start | bytes 589832 | tf_op jit(solution)/shard_map/ppermute | solution.py:128
  57.0 10.4 %collective-permute-start.17 = (bf16[128,384]{1,0:T(8,128)(2,1)S(1)}, bf16[128,384]{1,0:T(8,128)(2,1)S(1)}, u32[]{:S(2)}, u32[]{:S(2)}) collective-permute-start(bf16[128,384]{1,0:T(8,128)(2,1)S(1)} %broadcast_select_fusion.9), channel_id=1, source_target_pairs={{0,32},{8,40},{16,48},{24,56},{32,0},{40,8},{48,16},{56,24},{64,96... | collective-permute-start | bytes 294920 | tf_op jit(solution)/shard_map/ppermute | solution.py:128
  67.4 9.8 %collective-permute-start.18 = (bf16[64,384]{1,0:T(8,128)(2,1)S(1)}, bf16[64,384]{1,0:T(8,128)(2,1)S(1)}, u32[]{:S(2)}, u32[]{:S(2)}) collective-permute-start(bf16[64,384]{1,0:T(8,128)(2,1)S(1)} %broadcast_select_fusion.12), channel_id=1, source_target_pairs={{0,64},{8,72},{16,80},{24,88},{32,96},{40,104},{48,112},{56,120},{... | collective-permute-start | bytes 147464 | tf_op jit(solution)/shard_map/ppermute | solution.py:128
  77.2 9.6 %collective-permute-start.19 = (bf16[64,384]{1,0:T(8,128)(2,1)S(1)}, bf16[64,384]{1,0:T(8,128)(2,1)S(1)}, u32[]{:S(2)}, u32[]{:S(2)}) collective-permute-start(bf16[64,384]{1,0:T(8,128)(2,1)S(1)} %select_select_fusion.4), channel_id=1, source_target_pairs={{0,64},{8,72},{16,80},{24,88},{32,96},{40,104},{48,112},{56,120},{... | collective-permute-start | bytes 147464 | tf_op jit(solution)/shard_map/ppermute | solution.py:128
  82.6 47.7 %collective-permute-start.5 = (bf16[64,5120]{1,0:T(8,128)(2,1)S(1)}, bf16[64,5120]{1,0:T(8,128)(2,1)S(1)}, u32[]{:S(2)}, u32[]{:S(2)}) collective-permute-start(bf16[64,5120]{1,0:T(8,128)(2,1)S(1)} %slice.104), channel_id=1, source_target_pairs={{0,2},{1,3},{2,4},{3,5},{4,6},{5,7},{6,0},{7,1},{8,10},{9,11},{10,... | collective-permute-start | bytes 1966088 | tf_op jit(solution)/shard_map/ppermute | solution.py:38
  83.9 47.3 %collective-permute-start.6 = (bf16[64,5120]{1,0:T(8,128)(2,1)S(1)}, bf16[64,5120]{1,0:T(8,128)(2,1)S(1)}, u32[]{:S(2)}, u32[]{:S(2)}) collective-permute-start(bf16[64,5120]{1,0:T(8,128)(2,1)S(1)} %slice.105), channel_id=1, source_target_pairs={{0,6},{1,7},{2,0},{3,1},{4,2},{5,3},{6,4},{7,5},{8,14},{9,15},{10,... | collective-permute-start | bytes 1966088 | tf_op jit(solution)/shard_map/ppermute | solution.py:38
  84.8 40.8 %collective-permute-start.3 = (bf16[128,5120]{1,0:T(8,128)(2,1)}, bf16[128,5120]{1,0:T(8,128)(2,1)S(1)}, u32[]{:S(2)}, u32[]{:S(2)}) collective-permute-start(bf16[128,5120]{1,0:T(8,128)(2,1)} %collective-permute-done), channel_id=1, source_target_pairs={{0,2},{1,3},{2,4},{3,5},{4,6},{5,7},{6,0},{7,1},{8,10},{9,11},{10,... | collective-permute-start | bytes 3932168 | tf_op jit(solution)/shard_map/ppermute | solution.py:38
  86.0 40.9 %collective-permute-start.4 = (bf16[128,5120]{1,0:T(8,128)(2,1)}, bf16[128,5120]{1,0:T(8,128)(2,1)S(1)}, u32[]{:S(2)}, u32[]{:S(2)}) collective-permute-start(bf16[128,5120]{1,0:T(8,128)(2,1)} %collective-permute-done), channel_id=1, source_target_pairs={{0,6},{1,7},{2,0},{3,1},{4,2},{5,3},{6,4},{7,5},{8,14},{9,15},{10,... | collective-permute-start | bytes 3932168 | tf_op jit(solution)/shard_map/ppermute | solution.py:38
  93.2 10.6 %collective-permute-start.21 = (bf16[256,384]{1,0:T(8,128)(2,1)S(1)}, bf16[256,384]{1,0:T(8,128)(2,1)S(1)}, u32[]{:S(2)}, u32[]{:S(2)}) collective-permute-start(bf16[256,384]{1,0:T(8,128)(2,1)S(1)} %pad_maximum_fusion.2), channel_id=1, source_target_pairs={{0,16},{8,24},{16,0},{24,8},{32,48},{40,56},{48,32},{56,40},{64,80... | collective-permute-start | bytes 589832 | tf_op jit(solution)/shard_map/ppermute | solution.py:128
  114.4 80.9 %collective-permute-start.23 = (bf16[1024,384]{1,0:T(8,128)(2,1)}, bf16[1024,384]{1,0:T(8,128)(2,1)}, u32[]{:S(2)}, u32[]{:S(2)}) collective-permute-start(bf16[1024,384]{1,0:T(8,128)(2,1)} %pad_maximum_fusion.ck), channel_id=1, source_target_pairs={{0,8},{8,0},{16,24},{24,16},{32,40},{40,32},{48,56},{56,48},{64,72... | collective-permute-start | bytes 2359304 | tf_op jit(solution)/shard_map/ppermute | solution.py:31
  125.7 14.2 %collective-permute-start.7 = (bf16[64,5120]{1,0:T(8,128)(2,1)S(1)}, bf16[64,5120]{1,0:T(8,128)(2,1)S(1)}, u32[]{:S(2)}, u32[]{:S(2)}) collective-permute-start(bf16[64,5120]{1,0:T(8,128)(2,1)S(1)} %slice.106), channel_id=1, source_target_pairs={{0,2},{1,3},{2,4},{3,5},{4,6},{5,7},{6,0},{7,1},{8,10},{9,11},{10,... | collective-permute-start | bytes 1966088 | tf_op jit(solution)/shard_map/ppermute | solution.py:38
  127.0 13.9 %collective-permute-start.8 = (bf16[64,5120]{1,0:T(8,128)(2,1)S(1)}, bf16[64,5120]{1,0:T(8,128)(2,1)S(1)}, u32[]{:S(2)}, u32[]{:S(2)}) collective-permute-start(bf16[64,5120]{1,0:T(8,128)(2,1)S(1)} %slice.107), channel_id=1, source_target_pairs={{0,6},{1,7},{2,0},{3,1},{4,2},{5,3},{6,4},{7,5},{8,14},{9,15},{10,... | collective-permute-start | bytes 1966088 | tf_op jit(solution)/shard_map/ppermute | solution.py:38
  170.3 15.1 %collective-permute-start.11 = (f32[16,128]{1,0:T(8,128)}, f32[16,128]{1,0:T(8,128)S(1)}, u32[]{:S(2)}, u32[]{:S(2)}) collective-permute-start(f32[16,128]{1,0:T(8,128)} %fold.2.held), channel_id=1, source_target_pairs={{0,2},{1,3},{2,4},{3,5},{4,6},{5,7},{6,0},{7,1},{8,10},{9,11},{10,... | collective-permute-start | bytes 24584 | tf_op jit(solution)/shard_map/ppermute | solution.py:38
  172.9 12.5 %collective-permute-start.12 = (f32[16,128]{1,0:T(8,128)}, f32[16,128]{1,0:T(8,128)S(1)}, u32[]{:S(2)}, u32[]{:S(2)}) collective-permute-start(f32[16,128]{1,0:T(8,128)} %fold.2.held), channel_id=1, source_target_pairs={{0,6},{1,7},{2,0},{3,1},{4,2},{5,3},{6,4},{7,5},{8,14},{9,15},{10,... | collective-permute-start | bytes 24584 | tf_op jit(solution)/shard_map/ppermute | solution.py:38
  172.9 12.5 %collective-permute-start.13 = (f32[16,128]{1,0:T(8,128)}, f32[16,128]{1,0:T(8,128)S(1)}, u32[]{:S(2)}, u32[]{:S(2)}) collective-permute-start(f32[16,128]{1,0:T(8,128)} %fold.2.held), channel_id=1, source_target_pairs={{0,4},{1,5},{2,6},{3,7},{4,0},{5,1},{6,2},{7,3},{8,12},{9,13},{10,... | collective-permute-start | bytes 24584 | tf_op jit(solution)/shard_map/ppermute | solution.py:38
  183.4 17.4 %collective-permute-start.25 = (bf16[1024,384]{1,0:T(8,128)(2,1)}, bf16[1024,384]{1,0:T(8,128)(2,1)}, u32[]{:S(2)}, u32[]{:S(2)}) collective-permute-start(bf16[1024,384]{1,0:T(8,128)(2,1)} %add_convert_fusion.nv), channel_id=1, source_target_pairs={{0,8},{8,16},{16,24},{24,32},{32,40},{40,48},{48,56},{56,64},{64,7... | collective-permute-start | bytes 2359304 | tf_op jit(solution)/shard_map/ppermute | solution.py:44
  190.2 18.8 %collective-permute-start.24 = (bf16[1024,384]{1,0:T(8,128)(2,1)}, bf16[1024,384]{1,0:T(8,128)(2,1)S(1)}, u32[]{:S(2)}, u32[]{:S(2)}) collective-permute-start(bf16[1024,384]{1,0:T(8,128)(2,1)} %get-tuple-element.13.nk), channel_id=1, source_target_pairs={{0,8},{8,16},{16,24},{24,32},{32,40},{40,48},{48,56},{56,64},{64,7... | collective-permute-start | bytes 2359304 | tf_op jit(solution)/shard_map/ppermute | solution.py:44
  (22 other events, 140.1 us)
Sparse Core Ops, SparseCore 0:
  22.2 55.1 all-gather.4
  79.3 47.7 all-gather.2

commit v3 on v2

--- a/solution.py
+++ b/solution.py
@@ -128,7 +128,7 @@
     return lax.ppermute(value, "group", route)
 
 
-def spread_cache(cache_keys, cache_values, root):
+def spread_cache(cache_keys, cache_values, root, after):
     me = lax.axis_index("group")
     moves = (
         (0, lambda v: group_shift(v, dc=1)),
@@ -138,11 +138,13 @@
         (3, lambda v: swap_z(v, 4)),
     )
     low, high = cache_keys, cache_values
-    for bit, move in moves:
+    for n, (bit, move) in enumerate(moves):
         mine, theirs = (me >> bit) & 1, (root >> bit) & 1
         kept = jnp.where(mine == 1, high, low)
         sent = jnp.where(mine == 1, low, high)
         came = move(sent)
+        if n == 1:
+            came, _ = lax.optimization_barrier((came, after))
         held = jnp.where(mine == theirs, kept, came)
         half = held.shape[0] // 2
         low, high = held[:half], held[half:]
@@ -156,21 +158,29 @@
 
 
 def attend_kernel(
-    heads, scale, order, count, slots, query, ck, cv, ek, ev, nk, nv, out, keys, values, sems
+    heads, scale, order, count, slots, query, ck, cv, ek0, ek1, ev0, ev1, nk, nv, *rest
 ):
+    out, keys, values, sems = rest
     span = ck.shape[0]
-    tiles = span // TILE
+    tiles, half = span // TILE, span // 2
 
     def copies(parts):
         made = []
-        for n, (part, target) in enumerate(parts):
-            rows = pl.ds((n // 2) * span, span)
+        for n, (part, target, row) in enumerate(parts):
+            rows = pl.ds(row, part.shape[0])
             made.append(pltpu.make_async_copy(part, target.at[rows], sems.at[n]))
         return made
 
-    fresh = [(ek, keys), (ev, values), (nk, keys), (nv, values)]
-    straight = copies([(ck, keys), (cv, values)] + fresh)
-    crossed = copies([(cv, keys), (ck, values)] + fresh)
+    fresh = [
+        (ek0, keys, span),
+        (ek1, keys, span + half),
+        (ev0, values, span),
+        (ev1, values, span + half),
+        (nk, keys, 2 * span),
+        (nv, values, 2 * span),
+    ]
+    straight = copies([(ck, keys, 0), (cv, values, 0)] + fresh)
+    crossed = copies([(cv, keys, 0), (ck, values, 0)] + fresh)
 
     @pl.when(slots[tiles] == 0)
     def _():
@@ -187,11 +197,10 @@
     for copy in straight:
         copy.wait()
 
-    def few_tiles(first, pairs):
+    def all_heads(i, pairs):
         low = lax.broadcasted_iota(jnp.int32, (1, 2 * TILE), 1) < TILE
         for h in range(heads):
-            for i in (first, first + 1):
-                one_tile(h, i, pairs, low)
+            one_tile(h, i, pairs, low)
 
     def one_tile(h, i, pairs, low):
         from_row = pl.multiple_of(slots[i] * TILE, TILE)
@@ -230,10 +239,9 @@
         denominator = jnp.sum(total, axis=1, keepdims=True)
         out[pl.ds(to_row, TILE), cols] = (summed / denominator).astype(jnp.bfloat16)
 
-    @pl.loop(0, tiles // 2)
-    def _(step):
-        first = 2 * step
-        few_tiles(first, MOST // 2)
+    @pl.loop(0, tiles)
+    def _(i):
+        all_heads(i, MOST // 2)
 
 
 def attend(query, parts, order, count, slots, heads):
@@ -245,12 +253,12 @@
         grid_spec=pltpu.PrefetchScalarGridSpec(
             num_scalar_prefetch=3,
             grid=(),
-            in_specs=[whole] + [anywhere] * 6,
+            in_specs=[whole] + [anywhere] * len(parts),
             out_specs=whole,
             scratch_shapes=[
                 pltpu.VMEM((3 * rows, width), jnp.bfloat16),
                 pltpu.VMEM((3 * rows, width), jnp.bfloat16),
-                pltpu.SemaphoreType.DMA((6,)),
+                pltpu.SemaphoreType.DMA((len(parts),)),
             ],
         ),
         out_shape=jax.ShapeDtypeStruct((rows, width), jnp.bfloat16),
@@ -315,20 +323,22 @@
     modulated = modulate(latents, timesteps[0], mod_shift, mod_scale)
     swapped = jnp.concatenate([modulated[:, depth:], modulated[:, :depth]], axis=1)
     modulated = jnp.where(lax.axis_index("group") < NZ * NC, modulated, swapped)
-    tokens = jnp.concatenate(gather_tokens(modulated), axis=0)
+    blocks = gather_tokens(modulated)
+    tokens = jnp.concatenate(blocks, axis=0)
 
     def projected(first, last):
-        parts = [
-            jnp.dot(
-                tokens[:, n * depth : (n + 1) * depth],
-                w[:, first:last],
-                preferred_element_type=jnp.float32,
+        parts = []
+        for n, w in enumerate(weights):
+            parts.append(
+                jnp.dot(
+                    tokens[:, n * depth : (n + 1) * depth],
+                    w[:, first:last],
+                    preferred_element_type=jnp.float32,
+                )
             )
-            for n, w in enumerate(weights)
-        ]
         return parts[0] + parts[1]
 
-    held, crossed = spread_cache(cache_keys, cache_values, root)
+    held, crossed = spread_cache(cache_keys, cache_values, root, blocks[1])
     order, count, slots = tile_lists(
         tile_mask, lax.axis_index("group") == 0, lax.axis_index("tok")
     )
@@ -338,11 +348,16 @@
         [jnp.sum(raw_query * raw_query, axis=1), jnp.sum(raw_key * raw_key, axis=1)]
     )
     value_rows = projected(2 * head_cols, 3 * head_cols).astype(jnp.bfloat16)
-    earlier_values = from_behind(value_rows, "group", 1)
+    half = value_rows.shape[0] // 2
+    earlier_values = []
+    for n in range(2):
+        earlier_values.append(from_behind(value_rows[n * half : (n + 1) * half], "group", 1))
     key_rows = scaled_rows(raw_key, key_squares, width, key_gain)
-    earlier_keys = from_behind(key_rows, "group", 1)
+    earlier_keys = []
+    for n in range(2):
+        earlier_keys.append(from_behind(key_rows[n * half : (n + 1) * half], "group", 1))
     query_rows = scaled_rows(raw_query, query_squares, width, query_gain)
-    parts = (held, crossed, earlier_keys, earlier_values, key_rows, value_rows)
+    parts = (held, crossed, *earlier_keys, *earlier_values, key_rows, value_rows)
     return attend(query_rows, parts, order, count, slots, heads)
 
 

time: 232 us -> 246 us (1.060)
  the two profiles are of different devices: /device:TPU:28 before, /device:TPU:1 now
where the time goes in v3:
time: 246 us; the launch traced here: 243 us
  waiting for transfers between devices  74.1 us (30%)
  starting transfers between devices  63.1 us (26%)
  matrix products  28.3 us (12%)
  local copies, waits for them, and re-layouts  24.1 us (10%)
  other arithmetic  18.6 us (8%)
  Pallas kernels  17.6 us (7%)
  between operations  17.5 us (7%)
    ppermute x5, waiting for transfers between devices, group_shift(): return lax.ppermute(value, 'group', route)  43.4 us
    dot_general x4, matrix products, projected(): jnp.dot(tokens[:, n * depth:(n + 1) * depth], w[:, first:last], preferred...  28.3 us
    ppermute x6, starting transfers between devices, swap_z(): return lax.ppermute(value, 'group', route)  18.7 us
    ppermute x6, waiting for transfers between devices, swap_z(): return lax.ppermute(value, 'group', route)  18.3 us
    unnamed x48, local copies, waits for them, and re-layouts  16.2 us
    ppermute x13, starting transfers between devices, tok_shift(): return lax.ppermute(value, 'tok', route)  15.7 us
    pallas_call x1, Pallas kernels, attend(): pl.pallas_call(functools.partial(attend_kernel, heads, 1.0 / math.sqrt(wi...  14.9 us
    ppermute x4, starting transfers between devices, from_behind(): return lax.ppermute(block, axis, route)  14.4 us
  transfers between devices with their start and end apart: 30, of which 11 were waited for; matrix products, arithmetic and copies ran while one was open for 27% of the time, Pallas kernels for 1%

profile of v3, /device:TPU:1, one launch (start us, length us, event | category | flops | bytes accessed | tf_op | source)
XLA Modules:
  0.0 243.3 jit_solution(18140488217299350723)
XLA Ops:
  9.4 3.8 %collective-permute-start.9 = (bf16[160,1152]{1,0:T(8,128)(2,1)S(1)}, bf16[160,1152]{1,0:T(8,128)(2,1)S(1)}, u32[]{:S(2)}, u32[]{:S(2)}) collective-permute-start(bf16[160,1152]{1,0:T(8,128)(2,1)S(1)} %constant_dynamic-update-slice_fusion.10), channel_id=1, source_target_pairs={{0,128},{8,136},{16,144},{24,152},{32,160},{40,168},{48,176},{56,1... | collective-permute-start | bytes 1105928 | tf_op jit(solution)/shard_map/ppermute | solution.py:31
  13.2 7.3 %collective-permute-done.9 = bf16[160,1152]{1,0:T(8,128)(2,1)S(1)} collective-permute-done((bf16[160,1152]{1,0:T(8,128)(2,1)S(1)}, bf16[160,1152]{1,0:T(8,128)(2,1)S(1)}, u32[]{:S(2)}, u32[]{:S(2)}) %collective-permute-start.9) | collective-permute-done | bytes 368672 | tf_op jit(solution)/shard_map/ppermute | solution.py:31
  38.4 2.8 %collective-permute-start.15 = (bf16[512,384]{1,0:T(8,128)(2,1)S(1)}, bf16[512,384]{1,0:T(8,128)(2,1)S(1)}, u32[]{:S(2)}, u32[]{:S(2)}) collective-permute-start(bf16[512,384]{1,0:T(8,128)(2,1)S(1)} %broadcast_select_fusion.3), channel_id=1, source_target_pairs={{0,128},{8,136},{16,144},{24,152},{32,160},{40,168},{48,176},{56,1... | collective-permute-start | bytes 1179656 | tf_op jit(solution)/shard_map/ppermute | solution.py:31
  42.5 29.5 %collective-permute-done.15 = bf16[512,384]{1,0:T(8,128)(2,1)S(1)} collective-permute-done((bf16[512,384]{1,0:T(8,128)(2,1)S(1)}, bf16[512,384]{1,0:T(8,128)(2,1)S(1)}, u32[]{:S(2)}, u32[]{:S(2)}) %collective-permute-start.15) | collective-permute-done | bytes 393248 | tf_op jit(solution)/shard_map/ppermute | solution.py:31
  73.8 4.3 %collective-permute-done.16 = bf16[256,384]{1,0:T(8,128)(2,1)S(1)} collective-permute-done((bf16[256,384]{1,0:T(8,128)(2,1)S(1)}, bf16[256,384]{1,0:T(8,128)(2,1)S(1)}, u32[]{:S(2)}, u32[]{:S(2)}) %collective-permute-start.16) | collective-permute-done | bytes 196640 | tf_op jit(solution)/shard_map/ppermute | solution.py:128
  78.2 3.1 %collective-permute-start.17 = (bf16[128,384]{1,0:T(8,128)(2,1)S(1)}, bf16[128,384]{1,0:T(8,128)(2,1)S(1)}, u32[]{:S(2)}, u32[]{:S(2)}) collective-permute-start(bf16[128,384]{1,0:T(8,128)(2,1)S(1)} %broadcast_select_fusion.9), channel_id=1, source_target_pairs={{0,32},{8,40},{16,48},{24,56},{32,0},{40,8},{48,16},{56,24},{64,96... | collective-permute-start | bytes 294920 | tf_op jit(solution)/shard_map/ppermute | solution.py:128
  83.8 8.5 %collective-permute-start.18 = (bf16[64,384]{1,0:T(8,128)(2,1)S(1)}, bf16[64,384]{1,0:T(8,128)(2,1)S(1)}, u32[]{:S(2)}, u32[]{:S(2)}) collective-permute-start(bf16[64,384]{1,0:T(8,128)(2,1)S(1)} %broadcast_select_fusion.12), channel_id=1, source_target_pairs={{0,64},{8,72},{16,80},{24,88},{32,96},{40,104},{48,112},{56,120},{... | collective-permute-start | bytes 147464 | tf_op jit(solution)/shard_map/ppermute | solution.py:128
  95.1 5.2 %collective-permute-start.19 = (bf16[64,384]{1,0:T(8,128)(2,1)S(1)}, bf16[64,384]{1,0:T(8,128)(2,1)S(1)}, u32[]{:S(2)}, u32[]{:S(2)}) collective-permute-start(bf16[64,384]{1,0:T(8,128)(2,1)S(1)} %select_select_fusion.4), channel_id=1, source_target_pairs={{0,64},{8,72},{16,80},{24,88},{32,96},{40,104},{48,112},{56,120},{... | collective-permute-start | bytes 147464 | tf_op jit(solution)/shard_map/ppermute | solution.py:128
  104.9 2.7 %collective-permute-start.4 = (bf16[128,5120]{1,0:T(8,128)(2,1)}, bf16[128,5120]{1,0:T(8,128)(2,1)S(1)}, u32[]{:S(2)}, u32[]{:S(2)}) collective-permute-start(bf16[128,5120]{1,0:T(8,128)(2,1)} %collective-permute-done), channel_id=1, source_target_pairs={{0,6},{1,7},{2,0},{3,1},{4,2},{5,3},{6,4},{7,5},{8,14},{9,15},{10,... | collective-permute-start | bytes 3932168 | tf_op jit(solution)/shard_map/ppermute | solution.py:38
  107.7 2.5 %constant_dynamic-update-slice_fusion.8 = bf16[1024,5120]{1,0:T(8,128)(2,1)} fusion(bf16[1024,5120]{1,0:T(8,128)(2,1)} %get-tuple-element.9, bf16[128,5120]{1,0:T(8,128)(2,1)} %collective-permute-done), kind=kLoop, calls=%fused_computation.60 | loop fusion | bytes 2621440
  110.2 5.3 %collective-permute-done.20 = bf16[128,384]{1,0:T(8,128)(2,1)S(1)} collective-permute-done((bf16[128,384]{1,0:T(8,128)(2,1)S(1)}, bf16[128,384]{1,0:T(8,128)(2,1)S(1)}, u32[]{:S(2)}, u32[]{:S(2)}) %collective-permute-start.20) | collective-permute-done | bytes 98336 | tf_op jit(solution)/shard_map/ppermute | solution.py:128
  115.6 2.5 %constant_dynamic-update-slice_fusion.7 = bf16[1024,5120]{1,0:T(8,128)(2,1)} fusion(bf16[1024,5120]{1,0:T(8,128)(2,1)} %constant_dynamic-update-slice_fusion.8, bf16[128,5120]{1,0:T(8,128)(2,1)} %collective-permute-done.1), kind=kLoop, calls=%fused_computation.59 | loop fusion | bytes 2621440
  118.1 5.7 %collective-permute-done.21 = bf16[256,384]{1,0:T(8,128)(2,1)S(1)} collective-permute-done((bf16[256,384]{1,0:T(8,128)(2,1)S(1)}, bf16[256,384]{1,0:T(8,128)(2,1)S(1)}, u32[]{:S(2)}, u32[]{:S(2)}) %collective-permute-start.21) | collective-permute-done | bytes 196640 | tf_op jit(solution)/shard_map/ppermute | solution.py:128
  125.5 6.7 %collective-permute-done.22 = bf16[512,384]{1,0:T(8,128)(2,1)S(1)} collective-permute-done((bf16[512,384]{1,0:T(8,128)(2,1)S(1)}, bf16[512,384]{1,0:T(8,128)(2,1)S(1)}, u32[]{:S(2)}, u32[]{:S(2)}) %collective-permute-start.22) | collective-permute-done | bytes 393248 | tf_op jit(solution)/shard_map/ppermute | solution.py:31
  133.3 5.0 %collective-permute-start.23 = (bf16[1024,384]{1,0:T(8,128)(2,1)}, bf16[1024,384]{1,0:T(8,128)(2,1)}, u32[]{:S(2)}, u32[]{:S(2)}) collective-permute-start(bf16[1024,384]{1,0:T(8,128)(2,1)} %pad_maximum_fusion.ck), channel_id=1, source_target_pairs={{0,8},{8,0},{16,24},{24,16},{32,40},{40,32},{48,56},{56,48},{64,72... | collective-permute-start | bytes 2359304 | tf_op jit(solution)/shard_map/ppermute | solution.py:31
  138.3 4.9 %collective-permute-done.3 = bf16[128,5120]{1,0:T(8,128)(2,1)S(1)} collective-permute-done((bf16[128,5120]{1,0:T(8,128)(2,1)}, bf16[128,5120]{1,0:T(8,128)(2,1)S(1)}, u32[]{:S(2)}, u32[]{:S(2)}) %collective-permute-start.3) | collective-permute-done | bytes 1310752 | tf_op jit(solution)/shard_map/ppermute | solution.py:38
  143.4 2.7 %collective-permute-start.8 = (bf16[64,5120]{1,0:T(8,128)(2,1)S(1)}, bf16[64,5120]{1,0:T(8,128)(2,1)S(1)}, u32[]{:S(2)}, u32[]{:S(2)}) collective-permute-start(bf16[64,5120]{1,0:T(8,128)(2,1)S(1)} %slice.123), channel_id=1, source_target_pairs={{0,6},{1,7},{2,0},{3,1},{4,2},{5,3},{6,4},{7,5},{8,14},{9,15},{10,... | collective-permute-start | bytes 1966088 | tf_op jit(solution)/shard_map/ppermute | solution.py:38
  150.4 6.0 %collective-permute-done.7 = bf16[64,5120]{1,0:T(8,128)(2,1)S(1)} collective-permute-done((bf16[64,5120]{1,0:T(8,128)(2,1)S(1)}, bf16[64,5120]{1,0:T(8,128)(2,1)S(1)}, u32[]{:S(2)}, u32[]{:S(2)}) %collective-permute-start.7) | collective-permute-done | bytes 655392 | tf_op jit(solution)/shard_map/ppermute | solution.py:38
  158.2 9.6 %fusion.2 = f32[1024,768]{1,0:T(8,128)} fusion(bf16[1024,5120]{1,0:T(8,128)(2,1)} %constant_dynamic-update-slice_fusion, bf16[2560,1152]{1,0:T(8,128)(2,1)} %all-gather.5.cloned.1.call-done), kind=kOutput, calls=%fused_computation.2 | convolution fusion | flops 4026531840 | bytes 12320768 | tf_op jit(solution)/shard_map/dot_general | solution.py:333
  167.8 8.9 %fusion.19 = f32[1024,768]{1,0:T(8,128)S(1)} fusion(f32[1024,768]{1,0:T(8,128)} %fusion.2, bf16[2560,1152]{1,0:T(8,128)(2,1)} %all-gather.3.cloned.1.call-done, bf16[1024,5120]{1,0:T(8,128)(2,1)} %constant_dynamic-update-slice_fusion), kind=kOutput, calls=%fused_computation.21 | convolution fusion | flops 4027318272 | bytes 15466496 | tf_op jit(solution)/shard_map/dot_general | solution.py:333
  177.5 4.4 %fusion = f32[1024,384]{1,0:T(8,128)S(1)} fusion(bf16[1024,5120]{1,0:T(8,128)(2,1)S(1)} %copy-done.9, bf16[2560,1152]{1,0:T(8,128)(2,1)} %all-gather.5.cloned.1.call-done), kind=kOutput, calls=%fused_computation | convolution fusion | flops 2013265920 | bytes 8781824 | tf_op jit(solution)/shard_map/dot_general | solution.py:333
  181.9 5.3 %add_convert_fusion.nv = bf16[1024,384]{1,0:T(8,128)(2,1)} fusion(f32[1024,384]{1,0:T(8,128)S(1)} %fusion, bf16[2560,1152]{1,0:T(8,128)(2,1)} %all-gather.3.cloned.1.call-done, bf16[1024,5120]{1,0:T(8,128)(2,1)S(1)} %copy-done.9), kind=kOutput, calls=%fused_computation.22 | convolution fusion | flops 2014052352 | bytes 9568256 | tf_op jit(solution)/shard_map/dot_general | solution.py:333
  194.4 8.7 %collective-permute-start.26 = (bf16[512,384]{1,0:T(8,128)(2,1)}, bf16[512,384]{1,0:T(8,128)(2,1)S(1)}, u32[]{:S(2)}, u32[]{:S(2)}) collective-permute-start(bf16[512,384]{1,0:T(8,128)(2,1)} %get-tuple-element.20), channel_id=1, source_target_pairs={{0,8},{8,16},{16,24},{24,32},{32,40},{40,48},{48,56},{56,64},{64,7... | collective-permute-start | bytes 1179656 | tf_op jit(solution)/shard_map/ppermute | solution.py:44
  221.6 14.9 %attend.1 = bf16[1024,384]{1,0:T(8,128)(2,1)} custom-call(s32[192]{0:T(256)} %reshape.116.order, s32[24]{0:T(128)} %reshape.117.count, s32[9]{0:T(128)} %pad_add_fusion.1.slots, bf16[1024,384]{1,0:T(8,128)(2,1)} %get-tuple-element.16.query, bf16[1024,384]{1,0:T(8,128)(2,1)} %pad_maximum_fusion.ck, bf16[1024,384]{1,0:T(8,128)(2,1)} %collective-permute-done.23.cv, ...), custom_call_target="tpu_custom_call" | custom-call | flops 1610612736 | bytes 6291456 | tf_op jit(solution)/shard_map/attend/pallas_call | solution.py:251
  (146 shorter events, 65.5 us)
Async XLA Ops:
  6.5 151.7 %all-gather.5.cloned.1.call-start = ((), (), s32[]{:S(2)}) async-start(), calls=%async_computation.1 | async-start | bytes 6266880 | tf_op jit(solution)/shard_map/all_gather | solution.py:320
  9.4 11.1 %collective-permute-start.9 = (bf16[160,1152]{1,0:T(8,128)(2,1)S(1)}, bf16[160,1152]{1,0:T(8,128)(2,1)S(1)}, u32[]{:S(2)}, u32[]{:S(2)}) collective-permute-start(bf16[160,1152]{1,0:T(8,128)(2,1)S(1)} %constant_dynamic-update-slice_fusion.10), channel_id=1, source_target_pairs={{0,128},{8,136},{16,144},{24,152},{32,160},{40,168},{48,176},{56,1... | collective-permute-start | bytes 1105928 | tf_op jit(solution)/shard_map/ppermute | solution.py:31
  21.3 146.5 %all-gather.3.cloned.1.call-start = ((), (), s32[]{:S(2)}) async-start(), calls=%async_computation | async-start | bytes 6266880 | tf_op jit(solution)/shard_map/all_gather | solution.py:320
  23.5 13.4 %collective-permute-start.14 = (bf16[1024,384]{1,0:T(8,128)(2,1)}, bf16[1024,384]{1,0:T(8,128)(2,1)}, u32[]{:S(2)}, u32[]{:S(2)}) collective-permute-start(bf16[1024,384]{1,0:T(8,128)(2,1)} %broadcast_select_fusion), channel_id=1, source_target_pairs={{0,8},{8,0},{16,24},{24,16},{32,40},{40,32},{48,56},{56,48},{64,72... | collective-permute-start | bytes 2359304 | tf_op jit(solution)/shard_map/ppermute | solution.py:31
  30.5 41.5 %collective-permute-start = (bf16[128,5120]{1,0:T(8,128)(2,1)}, bf16[128,5120]{1,0:T(8,128)(2,1)}, u32[]{:S(2)}, u32[]{:S(2)}) collective-permute-start(bf16[128,5120]{1,0:T(8,128)(2,1)} %get-tuple-element.10), channel_id=1, source_target_pairs={{0,1},{1,0},{2,3},{3,2},{4,5},{5,4},{6,7},{7,6},{8,9},{9,8},{10,11... | collective-permute-start | bytes 3932168 | tf_op jit(solution)/shard_map/ppermute | solution.py:38
  31.8 69.0 %collective-permute-start.1 = (bf16[128,5120]{1,0:T(8,128)(2,1)}, bf16[128,5120]{1,0:T(8,128)(2,1)}, u32[]{:S(2)}, u32[]{:S(2)}) collective-permute-start(bf16[128,5120]{1,0:T(8,128)(2,1)} %get-tuple-element.10), channel_id=1, source_target_pairs={{0,2},{1,3},{2,4},{3,5},{4,6},{5,7},{6,0},{7,1},{8,10},{9,11},{10,... | collective-permute-start | bytes 3932168 | tf_op jit(solution)/shard_map/ppermute | solution.py:38
  33.1 70.2 %collective-permute-start.2 = (bf16[128,5120]{1,0:T(8,128)(2,1)}, bf16[128,5120]{1,0:T(8,128)(2,1)S(1)}, u32[]{:S(2)}, u32[]{:S(2)}) collective-permute-start(bf16[128,5120]{1,0:T(8,128)(2,1)} %get-tuple-element.10), channel_id=1, source_target_pairs={{0,6},{1,7},{2,0},{3,1},{4,2},{5,3},{6,4},{7,5},{8,14},{9,15},{10,... | collective-permute-start | bytes 3932168 | tf_op jit(solution)/shard_map/ppermute | solution.py:38
  38.4 33.6 %collective-permute-start.15 = (bf16[512,384]{1,0:T(8,128)(2,1)S(1)}, bf16[512,384]{1,0:T(8,128)(2,1)S(1)}, u32[]{:S(2)}, u32[]{:S(2)}) collective-permute-start(bf16[512,384]{1,0:T(8,128)(2,1)S(1)} %broadcast_select_fusion.3), channel_id=1, source_target_pairs={{0,128},{8,136},{16,144},{24,152},{32,160},{40,168},{48,176},{56,1... | collective-permute-start | bytes 1179656 | tf_op jit(solution)/shard_map/ppermute | solution.py:31
  83.8 11.3 %collective-permute-start.18 = (bf16[64,384]{1,0:T(8,128)(2,1)S(1)}, bf16[64,384]{1,0:T(8,128)(2,1)S(1)}, u32[]{:S(2)}, u32[]{:S(2)}) collective-permute-start(bf16[64,384]{1,0:T(8,128)(2,1)S(1)} %broadcast_select_fusion.12), channel_id=1, source_target_pairs={{0,64},{8,72},{16,80},{24,88},{32,96},{40,104},{48,112},{56,120},{... | collective-permute-start | bytes 147464 | tf_op jit(solution)/shard_map/ppermute | solution.py:128
  95.1 12.5 %collective-permute-start.19 = (bf16[64,384]{1,0:T(8,128)(2,1)S(1)}, bf16[64,384]{1,0:T(8,128)(2,1)S(1)}, u32[]{:S(2)}, u32[]{:S(2)}) collective-permute-start(bf16[64,384]{1,0:T(8,128)(2,1)S(1)} %select_select_fusion.4), channel_id=1, source_target_pairs={{0,64},{8,72},{16,80},{24,88},{32,96},{40,104},{48,112},{56,120},{... | collective-permute-start | bytes 147464 | tf_op jit(solution)/shard_map/ppermute | solution.py:128
  102.0 46.6 %collective-permute-start.5 = (bf16[64,5120]{1,0:T(8,128)(2,1)S(1)}, bf16[64,5120]{1,0:T(8,128)(2,1)S(1)}, u32[]{:S(2)}, u32[]{:S(2)}) collective-permute-start(bf16[64,5120]{1,0:T(8,128)(2,1)S(1)} %slice.120), channel_id=1, source_target_pairs={{0,2},{1,3},{2,4},{3,5},{4,6},{5,7},{6,0},{7,1},{8,10},{9,11},{10,... | collective-permute-start | bytes 1966088 | tf_op jit(solution)/shard_map/ppermute | solution.py:38
  103.4 46.2 %collective-permute-start.6 = (bf16[64,5120]{1,0:T(8,128)(2,1)S(1)}, bf16[64,5120]{1,0:T(8,128)(2,1)S(1)}, u32[]{:S(2)}, u32[]{:S(2)}) collective-permute-start(bf16[64,5120]{1,0:T(8,128)(2,1)S(1)} %slice.121), channel_id=1, source_target_pairs={{0,6},{1,7},{2,0},{3,1},{4,2},{5,3},{6,4},{7,5},{8,14},{9,15},{10,... | collective-permute-start | bytes 1966088 | tf_op jit(solution)/shard_map/ppermute | solution.py:38
  104.9 38.4 %collective-permute-start.3 = (bf16[128,5120]{1,0:T(8,128)(2,1)}, bf16[128,5120]{1,0:T(8,128)(2,1)S(1)}, u32[]{:S(2)}, u32[]{:S(2)}) collective-permute-start(bf16[128,5120]{1,0:T(8,128)(2,1)} %collective-permute-done), channel_id=1, source_target_pairs={{0,2},{1,3},{2,4},{3,5},{4,6},{5,7},{6,0},{7,1},{8,10},{9,11},{10,... | collective-permute-start | bytes 3932168 | tf_op jit(solution)/shard_map/ppermute | solution.py:38
  104.9 38.5 %collective-permute-start.4 = (bf16[128,5120]{1,0:T(8,128)(2,1)}, bf16[128,5120]{1,0:T(8,128)(2,1)S(1)}, u32[]{:S(2)}, u32[]{:S(2)}) collective-permute-start(bf16[128,5120]{1,0:T(8,128)(2,1)} %collective-permute-done), channel_id=1, source_target_pairs={{0,6},{1,7},{2,0},{3,1},{4,2},{5,3},{6,4},{7,5},{8,14},{9,15},{10,... | collective-permute-start | bytes 3932168 | tf_op jit(solution)/shard_map/ppermute | solution.py:38
  133.3 86.2 %collective-permute-start.23 = (bf16[1024,384]{1,0:T(8,128)(2,1)}, bf16[1024,384]{1,0:T(8,128)(2,1)}, u32[]{:S(2)}, u32[]{:S(2)}) collective-permute-start(bf16[1024,384]{1,0:T(8,128)(2,1)} %pad_maximum_fusion.ck), channel_id=1, source_target_pairs={{0,8},{8,0},{16,24},{24,16},{32,40},{40,32},{48,56},{56,48},{64,72... | collective-permute-start | bytes 2359304 | tf_op jit(solution)/shard_map/ppermute | solution.py:31
  143.3 13.1 %collective-permute-start.7 = (bf16[64,5120]{1,0:T(8,128)(2,1)S(1)}, bf16[64,5120]{1,0:T(8,128)(2,1)S(1)}, u32[]{:S(2)}, u32[]{:S(2)}) collective-permute-start(bf16[64,5120]{1,0:T(8,128)(2,1)S(1)} %slice.122), channel_id=1, source_target_pairs={{0,2},{1,3},{2,4},{3,5},{4,6},{5,7},{6,0},{7,1},{8,10},{9,11},{10,... | collective-permute-start | bytes 1966088 | tf_op jit(solution)/shard_map/ppermute | solution.py:38
  143.4 13.9 %collective-permute-start.8 = (bf16[64,5120]{1,0:T(8,128)(2,1)S(1)}, bf16[64,5120]{1,0:T(8,128)(2,1)S(1)}, u32[]{:S(2)}, u32[]{:S(2)}) collective-permute-start(bf16[64,5120]{1,0:T(8,128)(2,1)S(1)} %slice.123), channel_id=1, source_target_pairs={{0,6},{1,7},{2,0},{3,1},{4,2},{5,3},{6,4},{7,5},{8,14},{9,15},{10,... | collective-permute-start | bytes 1966088 | tf_op jit(solution)/shard_map/ppermute | solution.py:38
  177.1 10.1 %collective-permute-start.10 = (f32[16,128]{1,0:T(8,128)S(1)}, f32[16,128]{1,0:T(8,128)S(1)}, u32[]{:S(2)}, u32[]{:S(2)}) collective-permute-start(f32[16,128]{1,0:T(8,128)S(1)} %pad_maximum_fusion.4.held), channel_id=1, source_target_pairs={{0,1},{1,0},{2,3},{3,2},{4,5},{5,4},{6,7},{7,6},{8,9},{9,8},{10,11... | collective-permute-start | bytes 24584 | tf_op jit(solution)/shard_map/ppermute | solution.py:38
  189.1 13.9 %collective-permute-start.11 = (f32[16,128]{1,0:T(8,128)}, f32[16,128]{1,0:T(8,128)}, u32[]{:S(2)}, u32[]{:S(2)}) collective-permute-start(f32[16,128]{1,0:T(8,128)} %fold.2.held), channel_id=1, source_target_pairs={{0,2},{1,3},{2,4},{3,5},{4,6},{5,7},{6,0},{7,1},{8,10},{9,11},{10,... | collective-permute-start | bytes 24584 | tf_op jit(solution)/shard_map/ppermute | solution.py:38
  189.4 15.6 %collective-permute-start.12 = (f32[16,128]{1,0:T(8,128)}, f32[16,128]{1,0:T(8,128)}, u32[]{:S(2)}, u32[]{:S(2)}) collective-permute-start(f32[16,128]{1,0:T(8,128)} %fold.2.held), channel_id=1, source_target_pairs={{0,6},{1,7},{2,0},{3,1},{4,2},{5,3},{6,4},{7,5},{8,14},{9,15},{10,... | collective-permute-start | bytes 24584 | tf_op jit(solution)/shard_map/ppermute | solution.py:38
  191.8 13.2 %collective-permute-start.13 = (f32[16,128]{1,0:T(8,128)}, f32[16,128]{1,0:T(8,128)}, u32[]{:S(2)}, u32[]{:S(2)}) collective-permute-start(f32[16,128]{1,0:T(8,128)} %fold.2.held), channel_id=1, source_target_pairs={{0,4},{1,5},{2,6},{3,7},{4,0},{5,1},{6,2},{7,3},{8,12},{9,13},{10,... | collective-permute-start | bytes 24584 | tf_op jit(solution)/shard_map/ppermute | solution.py:38
  194.4 25.1 %collective-permute-start.26 = (bf16[512,384]{1,0:T(8,128)(2,1)}, bf16[512,384]{1,0:T(8,128)(2,1)S(1)}, u32[]{:S(2)}, u32[]{:S(2)}) collective-permute-start(bf16[512,384]{1,0:T(8,128)(2,1)} %get-tuple-element.20), channel_id=1, source_target_pairs={{0,8},{8,16},{16,24},{24,32},{32,40},{40,48},{48,56},{56,64},{64,7... | collective-permute-start | bytes 1179656 | tf_op jit(solution)/shard_map/ppermute | solution.py:44
  203.1 16.4 %collective-permute-start.27 = (bf16[512,384]{1,0:T(8,128)(2,1)}, bf16[512,384]{1,0:T(8,128)(2,1)}, u32[]{:S(2)}, u32[]{:S(2)}) collective-permute-start(bf16[512,384]{1,0:T(8,128)(2,1)} %get-tuple-element.19), channel_id=1, source_target_pairs={{0,8},{8,16},{16,24},{24,32},{32,40},{40,48},{48,56},{56,64},{64,7... | collective-permute-start | bytes 1179656 | tf_op jit(solution)/shard_map/ppermute | solution.py:44
  210.0 9.5 %collective-permute-start.24 = (bf16[512,384]{1,0:T(8,128)(2,1)S(1)}, bf16[512,384]{1,0:T(8,128)(2,1)S(1)}, u32[]{:S(2)}, u32[]{:S(2)}) collective-permute-start(bf16[512,384]{1,0:T(8,128)(2,1)S(1)} %get-tuple-element.22), channel_id=1, source_target_pairs={{0,8},{8,16},{16,24},{24,32},{32,40},{40,48},{48,56},{56,64},{64,7... | collective-permute-start | bytes 1179656 | tf_op jit(solution)/shard_map/ppermute | solution.py:44
  (25 other events, 224.6 us)
Sparse Core Ops, SparseCore 0:
  21.4 49.8 all-gather.4
  73.2 53.5 all-gather.2

commit v4 on v3

--- a/solution.py
+++ b/solution.py
@@ -158,11 +158,11 @@
 
 
 def attend_kernel(
-    heads, scale, order, count, slots, query, ck, cv, ek0, ek1, ev0, ev1, nk, nv, *rest
+    heads, scale, order, count, slots, query, ck, cv, ek, ev, nk, nv, *rest
 ):
     out, keys, values, sems = rest
     span = ck.shape[0]
-    tiles, half = span // TILE, span // 2
+    tiles = span // TILE
 
     def copies(parts):
         made = []
@@ -172,10 +172,8 @@
         return made
 
     fresh = [
-        (ek0, keys, span),
-        (ek1, keys, span + half),
-        (ev0, values, span),
-        (ev1, values, span + half),
+        (ek, keys, span),
+        (ev, values, span),
         (nk, keys, 2 * span),
         (nv, values, 2 * span),
     ]
@@ -311,7 +309,7 @@
     heads = tile_mask.shape[0]
     root = owners[owners.shape[0] - 1]
     modulated = modulate(latents, timesteps[0], mod_shift, mod_scale)
-    own_w = jnp.concatenate([w_query, w_key, w_value], axis=1)
+    own_w = lax.optimization_barrier(jnp.concatenate([w_query, w_key, w_value], axis=1))
     beside_w = group_shift(own_w, dy=1)
     planes = [[y * NZ * NC + n for n in range(NZ * NC)] for y in range(NY)]
     weights = []
@@ -348,16 +346,11 @@
         [jnp.sum(raw_query * raw_query, axis=1), jnp.sum(raw_key * raw_key, axis=1)]
     )
     value_rows = projected(2 * head_cols, 3 * head_cols).astype(jnp.bfloat16)
-    half = value_rows.shape[0] // 2
-    earlier_values = []
-    for n in range(2):
-        earlier_values.append(from_behind(value_rows[n * half : (n + 1) * half], "group", 1))
+    earlier_values = from_behind(value_rows, "group", 1)
     key_rows = scaled_rows(raw_key, key_squares, width, key_gain)
-    earlier_keys = []
-    for n in range(2):
-        earlier_keys.append(from_behind(key_rows[n * half : (n + 1) * half], "group", 1))
+    earlier_keys = from_behind(key_rows, "group", 1)
     query_rows = scaled_rows(raw_query, query_squares, width, query_gain)
-    parts = (held, crossed, *earlier_keys, *earlier_values, key_rows, value_rows)
+    parts = (held, crossed, earlier_keys, earlier_values, key_rows, value_rows)
     return attend(query_rows, parts, order, count, slots, heads)
 
 

time: 246 us -> 245 us (level)
  waiting for transfers between devices: 74.1 us -> 86.4 us
  local copies, waits for them, and re-layouts: 24.1 us -> 16.4 us
  starting transfers between devices: 63.1 us -> 57.1 us
  other arithmetic: 18.6 us -> 15.3 us
  matrix products: 28.3 us -> 31.5 us
    ppermute x4 -> x2, waiting for transfers between devices: 1.34 us -> 7.71 us  [from_behind(): return lax.ppermute(block, axis, route)]
    ppermute x6, waiting for transfers between devices: 18.3 us -> 23.3 us  [swap_z(): return lax.ppermute(value, 'group', route)]
    ppermute x4 -> x2, starting transfers between devices: 14.4 us -> 9.81 us  [from_behind(): return lax.ppermute(block, axis, route)]
    dot_general x4, matrix products: 28.3 us -> 31.5 us  [projected(): jnp.dot(tokens[:, n * depth:(n + 1) * depth], w[:, first:last], preferred...]
    unnamed x48 -> x44, local copies, waits for them, and re-layouts: 16.2 us -> 13.4 us
  transfers between devices with their start and end apart: 30 -> 28, of which waited for: 11 -> 11; matrix products, arithmetic and copies ran while one was open for 27% -> 24% of each run, Pallas kernels for 1% -> 1%
where the time goes in v4:
time: 245 us; the launch traced here: 242 us
  waiting for transfers between devices  86.4 us (35%)
  starting transfers between devices  57.1 us (23%)
  matrix products  31.5 us (13%)
  Pallas kernels  17.4 us (7%)
  between operations  17.3 us (7%)
  local copies, waits for them, and re-layouts  16.4 us (7%)
  other arithmetic  15.3 us (6%)
    ppermute x5, waiting for transfers between devices, group_shift(): return lax.ppermute(value, 'group', route)  45.1 us
    dot_general x4, matrix products, projected(): jnp.dot(tokens[:, n * depth:(n + 1) * depth], w[:, first:last], preferred...  31.5 us
    ppermute x6, waiting for transfers between devices, swap_z(): return lax.ppermute(value, 'group', route)  23.3 us
    ppermute x6, starting transfers between devices, swap_z(): return lax.ppermute(value, 'group', route)  18.1 us
    ppermute x13, starting transfers between devices, tok_shift(): return lax.ppermute(value, 'tok', route)  16.3 us
    pallas_call x1, Pallas kernels, attend(): pl.pallas_call(functools.partial(attend_kernel, heads, 1.0 / math.sqrt(wi...  14.8 us
    unnamed x44, local copies, waits for them, and re-layouts  13.4 us
    ppermute x5, starting transfers between devices, group_shift(): return lax.ppermute(value, 'group', route)  12.8 us
  transfers between devices with their start and end apart: 28, of which 11 were waited for; matrix products, arithmetic and copies ran while one was open for 24% of the time, Pallas kernels for 1%

profile of v4, /device:TPU:1, one launch (start us, length us, event | category | flops | bytes accessed | tf_op | source)
XLA Modules:
  0.0 241.5 jit_solution(8016979347898376585)
XLA Ops:
  7.7 3.8 %collective-permute-start.9 = (bf16[160,1152]{1,0:T(8,128)(2,1)S(1)}, bf16[160,1152]{1,0:T(8,128)(2,1)S(1)}, u32[]{:S(2)}, u32[]{:S(2)}) collective-permute-start(bf16[160,1152]{1,0:T(8,128)(2,1)S(1)} %pad_maximum_fusion.2), channel_id=1, source_target_pairs={{0,128},{8,136},{16,144},{24,152},{32,160},{40,168},{48,176},{56,1... | collective-permute-start | bytes 1105928 | tf_op jit(solution)/shard_map/ppermute | solution.py:31
  11.5 7.3 %collective-permute-done.9 = bf16[160,1152]{1,0:T(8,128)(2,1)S(1)} collective-permute-done((bf16[160,1152]{1,0:T(8,128)(2,1)S(1)}, bf16[160,1152]{1,0:T(8,128)(2,1)S(1)}, u32[]{:S(2)}, u32[]{:S(2)}) %collective-permute-start.9) | collective-permute-done | bytes 368672 | tf_op jit(solution)/shard_map/ppermute | solution.py:31
  33.4 2.6 %collective-permute-start.15 = (bf16[512,384]{1,0:T(8,128)(2,1)}, bf16[512,384]{1,0:T(8,128)(2,1)}, u32[]{:S(2)}, u32[]{:S(2)}) collective-permute-start(bf16[512,384]{1,0:T(8,128)(2,1)} %broadcast_select_fusion.3), channel_id=1, source_target_pairs={{0,128},{8,136},{16,144},{24,152},{32,160},{40,168},{48,176},{56,1... | collective-permute-start | bytes 1179656 | tf_op jit(solution)/shard_map/ppermute | solution.py:31
  40.5 29.9 %collective-permute-done.15 = bf16[512,384]{1,0:T(8,128)(2,1)} collective-permute-done((bf16[512,384]{1,0:T(8,128)(2,1)}, bf16[512,384]{1,0:T(8,128)(2,1)}, u32[]{:S(2)}, u32[]{:S(2)}) %collective-permute-start.15) | collective-permute-done | bytes 393248 | tf_op jit(solution)/shard_map/ppermute | solution.py:31
  72.2 4.3 %collective-permute-done.16 = bf16[256,384]{1,0:T(8,128)(2,1)S(1)} collective-permute-done((bf16[256,384]{1,0:T(8,128)(2,1)S(1)}, bf16[256,384]{1,0:T(8,128)(2,1)S(1)}, u32[]{:S(2)}, u32[]{:S(2)}) %collective-permute-start.16) | collective-permute-done | bytes 196640 | tf_op jit(solution)/shard_map/ppermute | solution.py:128
  76.6 3.1 %collective-permute-start.17 = (bf16[128,384]{1,0:T(8,128)(2,1)S(1)}, bf16[128,384]{1,0:T(8,128)(2,1)S(1)}, u32[]{:S(2)}, u32[]{:S(2)}) collective-permute-start(bf16[128,384]{1,0:T(8,128)(2,1)S(1)} %broadcast_select_fusion.9), channel_id=1, source_target_pairs={{0,32},{8,40},{16,48},{24,56},{32,0},{40,8},{48,16},{56,24},{64,96... | collective-permute-start | bytes 294920 | tf_op jit(solution)/shard_map/ppermute | solution.py:128
  79.7 2.8 %collective-permute-done.17 = bf16[128,384]{1,0:T(8,128)(2,1)S(1)} collective-permute-done((bf16[128,384]{1,0:T(8,128)(2,1)S(1)}, bf16[128,384]{1,0:T(8,128)(2,1)S(1)}, u32[]{:S(2)}, u32[]{:S(2)}) %collective-permute-start.17) | collective-permute-done | bytes 98336 | tf_op jit(solution)/shard_map/ppermute | solution.py:128
  82.6 8.4 %collective-permute-start.18 = (bf16[64,384]{1,0:T(8,128)(2,1)S(1)}, bf16[64,384]{1,0:T(8,128)(2,1)S(1)}, u32[]{:S(2)}, u32[]{:S(2)}) collective-permute-start(bf16[64,384]{1,0:T(8,128)(2,1)S(1)} %broadcast_select_fusion.12), channel_id=1, source_target_pairs={{0,64},{8,72},{16,80},{24,88},{32,96},{40,104},{48,112},{56,120},{... | collective-permute-start | bytes 147464 | tf_op jit(solution)/shard_map/ppermute | solution.py:128
  91.6 2.5 %collective-permute-done.18 = bf16[64,384]{1,0:T(8,128)(2,1)S(1)} collective-permute-done((bf16[64,384]{1,0:T(8,128)(2,1)S(1)}, bf16[64,384]{1,0:T(8,128)(2,1)S(1)}, u32[]{:S(2)}, u32[]{:S(2)}) %collective-permute-start.18) | collective-permute-done | bytes 49184 | tf_op jit(solution)/shard_map/ppermute | solution.py:128
  94.1 4.7 %collective-permute-start.19 = (bf16[64,384]{1,0:T(8,128)(2,1)S(1)}, bf16[64,384]{1,0:T(8,128)(2,1)S(1)}, u32[]{:S(2)}, u32[]{:S(2)}) collective-permute-start(bf16[64,384]{1,0:T(8,128)(2,1)S(1)} %select_select_fusion.4), channel_id=1, source_target_pairs={{0,64},{8,72},{16,80},{24,88},{32,96},{40,104},{48,112},{56,120},{... | collective-permute-start | bytes 147464 | tf_op jit(solution)/shard_map/ppermute | solution.py:128
  102.2 2.5 %collective-permute-start.4 = (bf16[128,5120]{1,0:T(8,128)(2,1)}, bf16[128,5120]{1,0:T(8,128)(2,1)S(1)}, u32[]{:S(2)}, u32[]{:S(2)}) collective-permute-start(bf16[128,5120]{1,0:T(8,128)(2,1)} %collective-permute-done), channel_id=1, source_target_pairs={{0,6},{1,7},{2,0},{3,1},{4,2},{5,3},{6,4},{7,5},{8,14},{9,15},{10,... | collective-permute-start | bytes 3932168 | tf_op jit(solution)/shard_map/ppermute | solution.py:38
  107.4 5.3 %collective-permute-done.20 = bf16[128,384]{1,0:T(8,128)(2,1)S(1)} collective-permute-done((bf16[128,384]{1,0:T(8,128)(2,1)S(1)}, bf16[128,384]{1,0:T(8,128)(2,1)S(1)}, u32[]{:S(2)}, u32[]{:S(2)}) %collective-permute-start.20) | collective-permute-done | bytes 98336 | tf_op jit(solution)/shard_map/ppermute | solution.py:128
  114.0 8.4 %collective-permute-done.21 = bf16[256,384]{1,0:T(8,128)(2,1)S(1)} collective-permute-done((bf16[256,384]{1,0:T(8,128)(2,1)S(1)}, bf16[256,384]{1,0:T(8,128)(2,1)S(1)}, u32[]{:S(2)}, u32[]{:S(2)}) %collective-permute-start.21) | collective-permute-done | bytes 196640 | tf_op jit(solution)/shard_map/ppermute | solution.py:128
  124.4 7.8 %collective-permute-done.22 = bf16[512,384]{1,0:T(8,128)(2,1)S(1)} collective-permute-done((bf16[512,384]{1,0:T(8,128)(2,1)S(1)}, bf16[512,384]{1,0:T(8,128)(2,1)S(1)}, u32[]{:S(2)}, u32[]{:S(2)}) %collective-permute-start.22) | collective-permute-done | bytes 393248 | tf_op jit(solution)/shard_map/ppermute | solution.py:31
  133.4 3.3 %collective-permute-start.23 = (bf16[1024,384]{1,0:T(8,128)(2,1)}, bf16[1024,384]{1,0:T(8,128)(2,1)}, u32[]{:S(2)}, u32[]{:S(2)}) collective-permute-start(bf16[1024,384]{1,0:T(8,128)(2,1)} %pad_maximum_fusion.ck), channel_id=1, source_target_pairs={{0,8},{8,0},{16,24},{24,16},{32,40},{40,32},{48,56},{56,48},{64,72... | collective-permute-start | bytes 2359304 | tf_op jit(solution)/shard_map/ppermute | solution.py:31
  136.7 4.2 %collective-permute-done.3 = bf16[128,5120]{1,0:T(8,128)(2,1)S(1)} collective-permute-done((bf16[128,5120]{1,0:T(8,128)(2,1)}, bf16[128,5120]{1,0:T(8,128)(2,1)S(1)}, u32[]{:S(2)}, u32[]{:S(2)}) %collective-permute-start.3) | collective-permute-done | bytes 1310752 | tf_op jit(solution)/shard_map/ppermute | solution.py:38
  148.1 6.0 %collective-permute-done.7 = bf16[64,5120]{1,0:T(8,128)(2,1)S(1)} collective-permute-done((bf16[64,5120]{1,0:T(8,128)(2,1)S(1)}, bf16[64,5120]{1,0:T(8,128)(2,1)S(1)}, u32[]{:S(2)}, u32[]{:S(2)}) %collective-permute-start.7) | collective-permute-done | bytes 655392 | tf_op jit(solution)/shard_map/ppermute | solution.py:38
  155.9 9.6 %fusion.2 = f32[1024,768]{1,0:T(8,128)} fusion(bf16[1024,5120]{1,0:T(8,128)(2,1)} %constant_dynamic-update-slice_fusion, bf16[2560,1152]{1,0:T(8,128)(2,1)} %all-gather.5.cloned.1.call-done), kind=kOutput, calls=%fused_computation.2 | convolution fusion | flops 4026531840 | bytes 12320768 | tf_op jit(solution)/shard_map/dot_general | solution.py:331
  165.5 8.9 %fusion.19 = f32[1024,768]{1,0:T(8,128)S(1)} fusion(f32[1024,768]{1,0:T(8,128)} %fusion.2, bf16[2560,1152]{1,0:T(8,128)(2,1)} %all-gather.3.cloned.1.call-done, bf16[1024,5120]{1,0:T(8,128)(2,1)} %constant_dynamic-update-slice_fusion), kind=kOutput, calls=%fused_computation.21 | convolution fusion | flops 4027318272 | bytes 15466496 | tf_op jit(solution)/shard_map/dot_general | solution.py:331
  175.1 5.6 %fusion = f32[1024,384]{1,0:T(8,128)} fusion(bf16[1024,5120]{1,0:T(8,128)(2,1)S(1)} %copy-done.6, bf16[2560,1152]{1,0:T(8,128)(2,1)} %all-gather.5.cloned.1.call-done), kind=kOutput, calls=%fused_computation | convolution fusion | flops 2013265920 | bytes 8781824 | tf_op jit(solution)/shard_map/dot_general | solution.py:331
  186.0 7.4 %add_convert_fusion.nv = bf16[1024,384]{1,0:T(8,128)(2,1)} fusion(f32[1024,384]{1,0:T(8,128)} %fusion, bf16[2560,1152]{1,0:T(8,128)(2,1)} %all-gather.3.cloned.1.call-done, bf16[1024,5120]{1,0:T(8,128)(2,1)} %constant_dynamic-update-slice_fusion), kind=kOutput, calls=%fused_computation.22 | convolution fusion | flops 2014052352 | bytes 9568256 | tf_op jit(solution)/shard_map/dot_general | solution.py:331
  193.5 7.9 %collective-permute-start.25 = (bf16[1024,384]{1,0:T(8,128)(2,1)}, bf16[1024,384]{1,0:T(8,128)(2,1)}, u32[]{:S(2)}, u32[]{:S(2)}) collective-permute-start(bf16[1024,384]{1,0:T(8,128)(2,1)} %add_convert_fusion.nv), channel_id=1, source_target_pairs={{0,8},{8,16},{16,24},{24,32},{32,40},{40,48},{48,56},{56,64},{64,7... | collective-permute-start | bytes 2359304 | tf_op jit(solution)/shard_map/ppermute | solution.py:44
  211.3 7.7 %collective-permute-done.24.ek = bf16[1024,384]{1,0:T(8,128)(2,1)S(1)} collective-permute-done((bf16[1024,384]{1,0:T(8,128)(2,1)}, bf16[1024,384]{1,0:T(8,128)(2,1)S(1)}, u32[]{:S(2)}, u32[]{:S(2)}) %collective-permute-start.24) | collective-permute-done | bytes 786464 | tf_op jit(solution)/shard_map/ppermute | solution.py:44
  219.9 14.8 %attend.1 = bf16[1024,384]{1,0:T(8,128)(2,1)} custom-call(s32[192]{0:T(256)} %reshape.116.order, s32[24]{0:T(128)} %reshape.117.count, s32[9]{0:T(128)} %pad_add_fusion.1.slots, bf16[1024,384]{1,0:T(8,128)(2,1)} %get-tuple-element.16.query, bf16[1024,384]{1,0:T(8,128)(2,1)} %pad_maximum_fusion.ck, bf16[1024,384]{1,0:T(8,128)(2,1)} %collective-permute-done.23.cv, ...), custom_call_target="tpu_custom_call" | custom-call | flops 1610612736 | bytes 6291456 | tf_op jit(solution)/shard_map/attend/pallas_call | solution.py:249
  (136 shorter events, 55.3 us)
Async XLA Ops:
  6.5 149.3 %all-gather.5.cloned.1.call-start = ((), (), s32[]{:S(2)}) async-start(), calls=%async_computation.1 | async-start | bytes 6266880 | tf_op jit(solution)/shard_map/all_gather | solution.py:318
  7.7 11.1 %collective-permute-start.9 = (bf16[160,1152]{1,0:T(8,128)(2,1)S(1)}, bf16[160,1152]{1,0:T(8,128)(2,1)S(1)}, u32[]{:S(2)}, u32[]{:S(2)}) collective-permute-start(bf16[160,1152]{1,0:T(8,128)(2,1)S(1)} %pad_maximum_fusion.2), channel_id=1, source_target_pairs={{0,128},{8,136},{16,144},{24,152},{32,160},{40,168},{48,176},{56,1... | collective-permute-start | bytes 1105928 | tf_op jit(solution)/shard_map/ppermute | solution.py:31
  19.6 145.9 %all-gather.3.cloned.1.call-start = ((), (), s32[]{:S(2)}) async-start(), calls=%async_computation | async-start | bytes 6266880 | tf_op jit(solution)/shard_map/all_gather | solution.py:318
  21.7 9.6 %collective-permute-start.14 = (bf16[1024,384]{1,0:T(8,128)(2,1)}, bf16[1024,384]{1,0:T(8,128)(2,1)}, u32[]{:S(2)}, u32[]{:S(2)}) collective-permute-start(bf16[1024,384]{1,0:T(8,128)(2,1)} %broadcast_select_fusion), channel_id=1, source_target_pairs={{0,8},{8,0},{16,24},{24,16},{32,40},{40,32},{48,56},{56,48},{64,72... | collective-permute-start | bytes 2359304 | tf_op jit(solution)/shard_map/ppermute | solution.py:31
  28.8 41.6 %collective-permute-start = (bf16[128,5120]{1,0:T(8,128)(2,1)}, bf16[128,5120]{1,0:T(8,128)(2,1)}, u32[]{:S(2)}, u32[]{:S(2)}) collective-permute-start(bf16[128,5120]{1,0:T(8,128)(2,1)} %get-tuple-element.10), channel_id=1, source_target_pairs={{0,1},{1,0},{2,3},{3,2},{4,5},{5,4},{6,7},{7,6},{8,9},{9,8},{10,11... | collective-permute-start | bytes 3932168 | tf_op jit(solution)/shard_map/ppermute | solution.py:38
  33.4 37.0 %collective-permute-start.15 = (bf16[512,384]{1,0:T(8,128)(2,1)}, bf16[512,384]{1,0:T(8,128)(2,1)}, u32[]{:S(2)}, u32[]{:S(2)}) collective-permute-start(bf16[512,384]{1,0:T(8,128)(2,1)} %broadcast_select_fusion.3), channel_id=1, source_target_pairs={{0,128},{8,136},{16,144},{24,152},{32,160},{40,168},{48,176},{56,1... | collective-permute-start | bytes 1179656 | tf_op jit(solution)/shard_map/ppermute | solution.py:31
  36.1 62.8 %collective-permute-start.1 = (bf16[128,5120]{1,0:T(8,128)(2,1)}, bf16[128,5120]{1,0:T(8,128)(2,1)S(1)}, u32[]{:S(2)}, u32[]{:S(2)}) collective-permute-start(bf16[128,5120]{1,0:T(8,128)(2,1)} %get-tuple-element.10), channel_id=1, source_target_pairs={{0,2},{1,3},{2,4},{3,5},{4,6},{5,7},{6,0},{7,1},{8,10},{9,11},{10,... | collective-permute-start | bytes 3932168 | tf_op jit(solution)/shard_map/ppermute | solution.py:38
  37.3 63.4 %collective-permute-start.2 = (bf16[128,5120]{1,0:T(8,128)(2,1)}, bf16[128,5120]{1,0:T(8,128)(2,1)S(1)}, u32[]{:S(2)}, u32[]{:S(2)}) collective-permute-start(bf16[128,5120]{1,0:T(8,128)(2,1)} %get-tuple-element.10), channel_id=1, source_target_pairs={{0,6},{1,7},{2,0},{3,1},{4,2},{5,3},{6,4},{7,5},{8,14},{9,15},{10,... | collective-permute-start | bytes 3932168 | tf_op jit(solution)/shard_map/ppermute | solution.py:38
  82.6 11.5 %collective-permute-start.18 = (bf16[64,384]{1,0:T(8,128)(2,1)S(1)}, bf16[64,384]{1,0:T(8,128)(2,1)S(1)}, u32[]{:S(2)}, u32[]{:S(2)}) collective-permute-start(bf16[64,384]{1,0:T(8,128)(2,1)S(1)} %broadcast_select_fusion.12), channel_id=1, source_target_pairs={{0,64},{8,72},{16,80},{24,88},{32,96},{40,104},{48,112},{56,120},{... | collective-permute-start | bytes 147464 | tf_op jit(solution)/shard_map/ppermute | solution.py:128
  94.1 10.7 %collective-permute-start.19 = (bf16[64,384]{1,0:T(8,128)(2,1)S(1)}, bf16[64,384]{1,0:T(8,128)(2,1)S(1)}, u32[]{:S(2)}, u32[]{:S(2)}) collective-permute-start(bf16[64,384]{1,0:T(8,128)(2,1)S(1)} %select_select_fusion.4), channel_id=1, source_target_pairs={{0,64},{8,72},{16,80},{24,88},{32,96},{40,104},{48,112},{56,120},{... | collective-permute-start | bytes 147464 | tf_op jit(solution)/shard_map/ppermute | solution.py:128
  98.9 47.3 %collective-permute-start.5 = (bf16[64,5120]{1,0:T(8,128)(2,1)S(1)}, bf16[64,5120]{1,0:T(8,128)(2,1)S(1)}, u32[]{:S(2)}, u32[]{:S(2)}) collective-permute-start(bf16[64,5120]{1,0:T(8,128)(2,1)S(1)} %slice.104), channel_id=1, source_target_pairs={{0,2},{1,3},{2,4},{3,5},{4,6},{5,7},{6,0},{7,1},{8,10},{9,11},{10,... | collective-permute-start | bytes 1966088 | tf_op jit(solution)/shard_map/ppermute | solution.py:38
  100.7 46.4 %collective-permute-start.6 = (bf16[64,5120]{1,0:T(8,128)(2,1)S(1)}, bf16[64,5120]{1,0:T(8,128)(2,1)S(1)}, u32[]{:S(2)}, u32[]{:S(2)}) collective-permute-start(bf16[64,5120]{1,0:T(8,128)(2,1)S(1)} %slice.105), channel_id=1, source_target_pairs={{0,6},{1,7},{2,0},{3,1},{4,2},{5,3},{6,4},{7,5},{8,14},{9,15},{10,... | collective-permute-start | bytes 1966088 | tf_op jit(solution)/shard_map/ppermute | solution.py:38
  102.1 38.8 %collective-permute-start.3 = (bf16[128,5120]{1,0:T(8,128)(2,1)}, bf16[128,5120]{1,0:T(8,128)(2,1)S(1)}, u32[]{:S(2)}, u32[]{:S(2)}) collective-permute-start(bf16[128,5120]{1,0:T(8,128)(2,1)} %collective-permute-done), channel_id=1, source_target_pairs={{0,2},{1,3},{2,4},{3,5},{4,6},{5,7},{6,0},{7,1},{8,10},{9,11},{10,... | collective-permute-start | bytes 3932168 | tf_op jit(solution)/shard_map/ppermute | solution.py:38
  102.2 39.2 %collective-permute-start.4 = (bf16[128,5120]{1,0:T(8,128)(2,1)}, bf16[128,5120]{1,0:T(8,128)(2,1)S(1)}, u32[]{:S(2)}, u32[]{:S(2)}) collective-permute-start(bf16[128,5120]{1,0:T(8,128)(2,1)} %collective-permute-done), channel_id=1, source_target_pairs={{0,6},{1,7},{2,0},{3,1},{4,2},{5,3},{6,4},{7,5},{8,14},{9,15},{10,... | collective-permute-start | bytes 3932168 | tf_op jit(solution)/shard_map/ppermute | solution.py:38
  112.7 9.6 %collective-permute-start.21 = (bf16[256,384]{1,0:T(8,128)(2,1)S(1)}, bf16[256,384]{1,0:T(8,128)(2,1)S(1)}, u32[]{:S(2)}, u32[]{:S(2)}) collective-permute-start(bf16[256,384]{1,0:T(8,128)(2,1)S(1)} %pad_maximum_fusion.3), channel_id=1, source_target_pairs={{0,16},{8,24},{16,0},{24,8},{32,48},{40,56},{48,32},{56,40},{64,80... | collective-permute-start | bytes 589832 | tf_op jit(solution)/shard_map/ppermute | solution.py:128
  122.5 9.8 %collective-permute-start.22 = (bf16[512,384]{1,0:T(8,128)(2,1)S(1)}, bf16[512,384]{1,0:T(8,128)(2,1)S(1)}, u32[]{:S(2)}, u32[]{:S(2)}) collective-permute-start(bf16[512,384]{1,0:T(8,128)(2,1)S(1)} %pad_maximum_fusion.1), channel_id=1, source_target_pairs={{0,128},{8,136},{16,144},{24,152},{32,160},{40,168},{48,176},{56,1... | collective-permute-start | bytes 1179656 | tf_op jit(solution)/shard_map/ppermute | solution.py:31
  133.4 77.9 %collective-permute-start.23 = (bf16[1024,384]{1,0:T(8,128)(2,1)}, bf16[1024,384]{1,0:T(8,128)(2,1)}, u32[]{:S(2)}, u32[]{:S(2)}) collective-permute-start(bf16[1024,384]{1,0:T(8,128)(2,1)} %pad_maximum_fusion.ck), channel_id=1, source_target_pairs={{0,8},{8,0},{16,24},{24,16},{32,40},{40,32},{48,56},{56,48},{64,72... | collective-permute-start | bytes 2359304 | tf_op jit(solution)/shard_map/ppermute | solution.py:31
  141.0 13.1 %collective-permute-start.7 = (bf16[64,5120]{1,0:T(8,128)(2,1)S(1)}, bf16[64,5120]{1,0:T(8,128)(2,1)S(1)}, u32[]{:S(2)}, u32[]{:S(2)}) collective-permute-start(bf16[64,5120]{1,0:T(8,128)(2,1)S(1)} %slice.106), channel_id=1, source_target_pairs={{0,2},{1,3},{2,4},{3,5},{4,6},{5,7},{6,0},{7,1},{8,10},{9,11},{10,... | collective-permute-start | bytes 1966088 | tf_op jit(solution)/shard_map/ppermute | solution.py:38
  141.5 13.5 %collective-permute-start.8 = (bf16[64,5120]{1,0:T(8,128)(2,1)S(1)}, bf16[64,5120]{1,0:T(8,128)(2,1)S(1)}, u32[]{:S(2)}, u32[]{:S(2)}) collective-permute-start(bf16[64,5120]{1,0:T(8,128)(2,1)S(1)} %slice.107), channel_id=1, source_target_pairs={{0,6},{1,7},{2,0},{3,1},{4,2},{5,3},{6,4},{7,5},{8,14},{9,15},{10,... | collective-permute-start | bytes 1966088 | tf_op jit(solution)/shard_map/ppermute | solution.py:38
  182.6 18.8 %collective-permute-start.11 = (f32[16,128]{1,0:T(8,128)}, f32[16,128]{1,0:T(8,128)S(1)}, u32[]{:S(2)}, u32[]{:S(2)}) collective-permute-start(f32[16,128]{1,0:T(8,128)} %fold.2.held), channel_id=1, source_target_pairs={{0,2},{1,3},{2,4},{3,5},{4,6},{5,7},{6,0},{7,1},{8,10},{9,11},{10,... | collective-permute-start | bytes 24584 | tf_op jit(solution)/shard_map/ppermute | solution.py:38
  183.2 18.2 %collective-permute-start.12 = (f32[16,128]{1,0:T(8,128)}, f32[16,128]{1,0:T(8,128)S(1)}, u32[]{:S(2)}, u32[]{:S(2)}) collective-permute-start(f32[16,128]{1,0:T(8,128)} %fold.2.held), channel_id=1, source_target_pairs={{0,6},{1,7},{2,0},{3,1},{4,2},{5,3},{6,4},{7,5},{8,14},{9,15},{10,... | collective-permute-start | bytes 24584 | tf_op jit(solution)/shard_map/ppermute | solution.py:38
  185.3 16.1 %collective-permute-start.13 = (f32[16,128]{1,0:T(8,128)}, f32[16,128]{1,0:T(8,128)S(1)}, u32[]{:S(2)}, u32[]{:S(2)}) collective-permute-start(f32[16,128]{1,0:T(8,128)} %fold.2.held), channel_id=1, source_target_pairs={{0,4},{1,5},{2,6},{3,7},{4,0},{5,1},{6,2},{7,3},{8,12},{9,13},{10,... | collective-permute-start | bytes 24584 | tf_op jit(solution)/shard_map/ppermute | solution.py:38
  193.5 17.9 %collective-permute-start.25 = (bf16[1024,384]{1,0:T(8,128)(2,1)}, bf16[1024,384]{1,0:T(8,128)(2,1)}, u32[]{:S(2)}, u32[]{:S(2)}) collective-permute-start(bf16[1024,384]{1,0:T(8,128)(2,1)} %add_convert_fusion.nv), channel_id=1, source_target_pairs={{0,8},{8,16},{16,24},{24,32},{32,40},{40,48},{48,56},{56,64},{64,7... | collective-permute-start | bytes 2359304 | tf_op jit(solution)/shard_map/ppermute | solution.py:44
  206.2 12.8 %collective-permute-start.24 = (bf16[1024,384]{1,0:T(8,128)(2,1)}, bf16[1024,384]{1,0:T(8,128)(2,1)S(1)}, u32[]{:S(2)}, u32[]{:S(2)}) collective-permute-start(bf16[1024,384]{1,0:T(8,128)(2,1)} %get-tuple-element.15.nk), channel_id=1, source_target_pairs={{0,8},{8,16},{16,24},{24,32},{32,40},{40,48},{48,56},{56,64},{64,7... | collective-permute-start | bytes 2359304 | tf_op jit(solution)/shard_map/ppermute | solution.py:44
  (22 other events, 166.5 us)
Sparse Core Ops, SparseCore 0:
  19.7 49.8 all-gather.4
  71.4 54.2 all-gather.2
